TPU v7x, 256 devices: a whole 4x4x8 slice. The times are simulated.
256 devices in a mesh: gy: 32 (over z, y), gx: 8 (over x, core).
Axes of the slice: x: 4, y: 4, z: 8, core: 2. Of those that a mesh axis runs over, the one named last changes fastest.
Arguments:
- bins: int32 [4, 512, 8192], P(None, 'gy', 'gx'), may hold values from 0 to 4095
- mask: int32 [4, 512, 8192], P(None, 'gy', 'gx'), may hold values from 0 to 1
- atlas: bfloat16 [8, 4, 512, 8192], P(None, None, 'gy', 'gx'), may hold values from -100 to 130
- init_mean: float32 [8], replicated, may hold values from 0.05 to 0.95
- init_scale: float32 [8], replicated, may hold values from 0.004 to 0.15
Outputs:
- phase_prob: bfloat16 [8, 4, 512, 8192], P(None, None, 'gy', 'gx')
- em_params: float32 [3, 8], replicated
- bin_density: float32 [4096], P(('gy', 'gx'))
All inputs are finite; a program needn't handle non-finite values.
Results may differ from a plain program's by a relative error of at most 0.0015.
Values may be sent and summed in bfloat16 or wider, within the bound.
A program may use at most 64 MiB of HBM per device.

v0:
```python
import math

import jax
import jax.numpy as jnp
from jax import lax
from jax.sharding import PartitionSpec as P

NB = 4096
EM_ITERS = 5
POTTS = 3


VAR_EPS = 1e-05
BETA = 0.3


def extended(x, sides, width):
    for axis, dim in sides:
        size, length = (lax.axis_size(axis), x.shape[dim])
        up = [(i, (i + 1) % size) for i in range(size - 1)]
        down = [(j, i) for i, j in up]
        last = lax.slice_in_dim(x, length - width, length, axis=dim)
        initial = lax.slice_in_dim(x, 0, width, axis=dim)
        before = lax.ppermute(last, axis, up)
        after = lax.ppermute(initial, axis, down)
        x = jnp.concatenate([before, x, after], axis=dim)
    return x


def phase_scores(values, mean, var, weight):
    shape = (mean.shape[0],) + (1,) * values.ndim
    m = mean.reshape(shape)
    v = var.reshape(shape)
    w = weight.reshape(shape)
    diff = values[None] - m
    return jnp.log(w) - 0.5 * jnp.log(v) - diff * diff / (2.0 * v)


def moments(counts, centers, mean, var, weight):
    resp = jax.nn.softmax(phase_scores(centers, mean, var, weight), axis=0)
    weighted = resp * counts[None]
    return jnp.stack(
        [
            jnp.sum(weighted, 1),
            jnp.sum(weighted * centers[None], 1),
            jnp.sum(weighted * (centers * centers)[None], 1),
        ]
    )


def refit(sums, count_phases):
    occ, first, second = (sums[0], sums[1], sums[2])
    mean = first / (occ + 1.0)
    var = (second - first * mean) / (occ + 1.0) + VAR_EPS
    weight = (occ + 1.0) / (jnp.sum(occ) + count_phases)
    return (mean, var, weight)


def cycle_total(padded, rows, cols):
    total = jnp.zeros(padded.shape[:2] + (rows, cols), jnp.float32)
    for dy in range(-2, 3):
        for dx in range(-2, 3):
            if dy != 0 or dx != 0:
                piece = padded[:, :, 2 + dy : 2 + dy + rows, 2 + dx : 2 + dx + cols].astype(
                    jnp.float32
                )
                total = total + piece * (1.0 / (dy * dy + dx * dx))
    return total


def plane_total(held):
    padded = jnp.pad(held.astype(jnp.float32), ((0, 0), (1, 1), (0, 0), (0, 0)))
    return padded[:, :-2] + padded[:, 2:]


def per_device(bins, mask, atlas, init_mean, init_scale):
    planes, rows, cols = bins.shape
    phases = init_mean.shape[0]
    devices_all = lax.axis_size("gy") * lax.axis_size("gx")
    scale_factor = float(NB) / float(planes * rows * cols * devices_all)
    group = math.gcd(16, planes * rows)
    block_bins = bins.reshape(-1, group * cols)
    block_mask = mask.reshape(-1, group * cols)
    high_count = NB // 128

    def count_block(acc, item):
        part_bins, part_mask = item
        high = part_bins // 128
        low = part_bins % 128
        high_hot = (high[None, :] == jnp.arange(high_count, dtype=jnp.int32)[:, None]).astype(
            jnp.bfloat16
        )
        high_hot = high_hot * part_mask.astype(jnp.bfloat16)[None, :]
        low_hot = (low[None, :] == jnp.arange(128, dtype=jnp.int32)[:, None]).astype(jnp.bfloat16)
        table = lax.dot_general(
            high_hot, low_hot, (((1,), (1,)), ((), ())), preferred_element_type=jnp.float32
        )
        return (acc + table, None)

    table, _ = lax.scan(
        count_block, jnp.zeros((high_count, 128), jnp.float32), (block_bins, block_mask)
    )
    counts = table.reshape(NB)
    mean = init_mean
    var = init_scale * init_scale
    weight = jnp.full((phases,), 1.0 / phases, jnp.float32)
    share = lax.psum_scatter(counts, ("gy", "gx"), scatter_dimension=0, tiled=True)
    start = lax.axis_index(("gy", "gx")) * share.shape[0]
    density = share * scale_factor
    centers = ((start + jnp.arange(share.shape[0], dtype=jnp.int32)).astype(jnp.float32) + 0.5) / NB
    for step in range(EM_ITERS):
        sums = lax.psum(moments(share, centers, mean, var, weight), ("gy", "gx"))
        mean, var, weight = refit(sums, float(phases))
    params = jnp.stack([mean, var, weight])
    intensity = (bins.astype(jnp.float32) + 0.5) / NB
    unary = phase_scores(intensity, mean, var, weight) + atlas.astype(jnp.float32)
    fg = mask.astype(jnp.float32)
    q = jax.nn.softmax(unary, axis=0).astype(jnp.bfloat16)
    for step in range(POTTS):
        held = (q.astype(jnp.float32) * fg[None]).astype(jnp.bfloat16)
        padded = extended(held, (("gy", 2), ("gx", 3)), 2)
        field = cycle_total(padded, rows, cols) + plane_total(held)
        q = jax.nn.softmax(unary + BETA * field, axis=0).astype(jnp.bfloat16)
    phase_prob = (q.astype(jnp.float32) * fg[None]).astype(jnp.bfloat16)
    return (phase_prob, params, density)


def solution(mesh):
    in_specs = (P(None, "gy", "gx"), P(None, "gy", "gx"), P(None, None, "gy", "gx"), P(), P())
    out_specs = (P(None, None, "gy", "gx"), P(), P(("gy", "gx")))
    return jax.shard_map(
        per_device, mesh=mesh, in_specs=in_specs, out_specs=out_specs, check_vma=False
    )
```

profile of v0, /device:TPU:1, one launch (start us, length us, event | category | flops | bytes accessed | tf_op | source)
XLA Modules:
  0.0 583.8 jit_solution(10782457312624884916)
XLA Ops:
  0.7 0.7 multiply_subtract_fusion
  1.3 0.7 fusion.37
  2.1 0.7 fusion.28
  2.8 1.1 copy.9
  4.0 1.1 copy.8
  5.1 10.4 %while.13 = (s32[]{:T(128)}, f32[32,128]{1,0:T(8,128)S(1)}, s32[4,16384]{1,0:T(4,128)S(1)}, s32[4,16384]{1,0:T(4,128)S(1)}, s32[]{:T(128)}, /*index=5*/s32[]{:T(128)}) while((s32[]{:T(128)}, f32[32,128]{1,0:T(8,128)S(1)}, s32[4,16384]{1,0:T(4,128)S(1)}, s32[4,16384]{1,0:T(4,128)S(1)}, s32[]{:T(128)}, /*index=5*/s32[]{:T(128)}) %tuple.78), condition=%wide.region_3.4_spmd.clone, body=%wide.region_2.3_spmd.clone.sunk | while | flops 137715712 | bytes 2719839 | solution.py:100
  5.4 0.3 and_select_fusion.4
  6.0 1.7 fusion.95
  8.0 0.3 and_select_fusion.4
  8.6 1.7 fusion.95
  10.6 0.3 and_select_fusion.4
  11.2 1.7 fusion.95
  13.1 0.3 and_select_fusion.4
  13.8 1.7 fusion.95
  15.5 81.5 %all-reduce.3 = f32[4096]{0:T(1024)S(1)} all-reduce(f32[4096]{0:T(1024)S(1)} %bitcast.175), channel_id=2, replica_groups=mesh['gy'=32,'gx'=8] {'gy','gx'}, use_global_device_ids=true, to_apply=%region_4.5.clone | all-reduce | flops 4096 | bytes 32768
  97.0 0.6 broadcast_multiply_fusion.5
  97.8 72.3 %psum.35 = f32[3,8]{1,0:T(4,128)S(1)} all-reduce(f32[3,8]{1,0:T(4,128)S(1)} %pad_maximum_fusion.18), channel_id=1, replica_groups=mesh['gy'=32,'gx'=8] {'gy','gx'}, use_global_device_ids=true, to_apply=%region_8.9 | all-reduce | flops 24 | bytes 192 | tf_op jit(solution)/shard_map/psum | solution.py:112
  170.2 0.6 slice_reduce_fusion.4
  171.9 73.7 %psum.36 = f32[3,8]{1,0:T(4,128)S(1)} all-reduce(f32[3,8]{1,0:T(4,128)S(1)} %pad_maximum_fusion.19), channel_id=1, replica_groups=mesh['gy'=32,'gx'=8] {'gy','gx'}, use_global_device_ids=true, to_apply=%region_15.16 | all-reduce | flops 24 | bytes 192 | tf_op jit(solution)/shard_map/psum | solution.py:112
  245.6 0.6 slice_reduce_fusion.3
  247.3 73.5 %psum.37 = f32[3,8]{1,0:T(4,128)S(1)} all-reduce(f32[3,8]{1,0:T(4,128)S(1)} %pad_maximum_fusion.20), channel_id=1, replica_groups=mesh['gy'=32,'gx'=8] {'gy','gx'}, use_global_device_ids=true, to_apply=%region_22.23 | all-reduce | flops 24 | bytes 192 | tf_op jit(solution)/shard_map/psum | solution.py:112
  320.7 0.6 slice_reduce_fusion.2
  322.5 74.2 %psum.38 = f32[3,8]{1,0:T(4,128)S(1)} all-reduce(f32[3,8]{1,0:T(4,128)S(1)} %pad_maximum_fusion.21), channel_id=1, replica_groups=mesh['gy'=32,'gx'=8] {'gy','gx'}, use_global_device_ids=true, to_apply=%region_29.30 | all-reduce | flops 24 | bytes 192 | tf_op jit(solution)/shard_map/psum | solution.py:112
  396.6 0.6 slice_reduce_fusion.1
  398.4 73.5 %psum.39 = f32[3,8]{1,0:T(4,128)S(1)} all-reduce(f32[3,8]{1,0:T(4,128)S(1)} %pad_maximum_fusion.22), channel_id=1, replica_groups=mesh['gy'=32,'gx'=8] {'gy','gx'}, use_global_device_ids=true, to_apply=%region_36.37 | all-reduce | flops 24 | bytes 192 | tf_op jit(solution)/shard_map/psum | solution.py:112
  471.9 0.6 fusion.63
  473.2 0.6 fusion.70
  473.8 0.7 fusion.18
  474.5 0.9 multiply_convert_fusion.3
  475.7 2.6 collective-permute-start
  478.3 1.3 collective-permute-start.1
  479.6 0.9 collective-permute-done
  480.4 3.6 collective-permute-done.1
  484.2 3.3 collective-permute-start.2
  487.5 2.2 collective-permute-start.3
  489.7 0.4 pad_convert_fusion.2
  490.1 4.4 collective-permute-done.3
  494.5 2.9 maximum_maximum_fusion
  497.4 11.3 %fusion.75 = (f32[4,16,1024]{2,1,0:T(8,128)S(1)}, f32[8,4,16,1024]{3,2,1,0:T(8,128)S(1)}) fusion(f32[8,6,16,1024]{3,2,1,0:T(8,128)S(1)} %pad_convert_fusion.2, bf16[8,4,20,1026]{3,2,1,0:T(8,128)(2,1)S(1)} %get-tuple-element.134, bf16[8,4,2,1024]{3,2,1,0:T(2,128)(2,1)S(1)} %collective-permute-done.1, bf16[8,4,16,1024]{3,2,1,0:T(8,128)(2,1)S(1)} %multiply_convert_fusion.3, ...), kind=kLoop, calls=%fused_computation.201 | loop fusion | flops 47120384 | bytes 30146656 | tf_op jit(solution)/shard_map/reduce_max | solution.py:123
  508.7 0.3 fusion.19
  509.0 0.4 multiply_convert_fusion.2
  509.6 3.6 collective-permute-start.4
  513.3 1.3 collective-permute-start.5
  514.6 0.6 collective-permute-done.4
  515.2 4.8 collective-permute-done.5
  520.2 3.9 collective-permute-start.6
  524.2 1.9 collective-permute-start.7
  526.1 0.4 pad_convert_fusion.1
  526.7 4.4 collective-permute-done.7
  531.1 2.9 maximum_maximum_fusion.1
  534.0 11.3 %fusion.73 = (f32[4,16,1024]{2,1,0:T(8,128)S(1)}, f32[8,4,16,1024]{3,2,1,0:T(8,128)S(1)}) fusion(f32[8,6,16,1024]{3,2,1,0:T(8,128)S(1)} %pad_convert_fusion.1, bf16[8,4,20,1026]{3,2,1,0:T(8,128)(2,1)S(1)} %get-tuple-element.130, bf16[8,4,2,1024]{3,2,1,0:T(2,128)(2,1)S(1)} %collective-permute-done.5, bf16[8,4,16,1024]{3,2,1,0:T(8,128)(2,1)S(1)} %multiply_convert_fusion.2, ...), kind=kLoop, calls=%fused_computation.200 | loop fusion | flops 47120384 | bytes 30146656 | tf_op jit(solution)/shard_map/reduce_max | solution.py:123
  545.3 0.3 fusion.20
  545.6 0.4 multiply_convert_fusion.1
  546.3 5.5 collective-permute-start.8
  551.8 1.3 collective-permute-start.9
  553.1 0.6 pad_maximum_fusion.23
  553.7 3.8 collective-permute-done.9
  557.7 3.2 collective-permute-start.10
  561.0 2.1 collective-permute-start.11
  563.1 0.4 pad_convert_fusion
  563.6 4.4 collective-permute-done.11
  568.0 2.9 maximum_maximum_fusion.2
  570.9 11.3 %fusion.71 = (f32[4,16,1024]{2,1,0:T(8,128)S(1)}, f32[8,4,16,1024]{3,2,1,0:T(8,128)S(1)}) fusion(f32[8,6,16,1024]{3,2,1,0:T(8,128)S(1)} %pad_convert_fusion, bf16[8,4,20,1026]{3,2,1,0:T(8,128)(2,1)S(1)} %get-tuple-element.126, bf16[8,4,2,1024]{3,2,1,0:T(2,128)(2,1)S(1)} %collective-permute-done.9, bf16[8,4,16,1024]{3,2,1,0:T(8,128)(2,1)S(1)} %multiply_convert_fusion.1, ...), kind=kLoop, calls=%fused_computation.199 | loop fusion | flops 47120384 | bytes 30146656 | tf_op jit(solution)/shard_map/reduce_max | solution.py:123
  582.4 1.4 multiply_convert_fusion
  (64 shorter events, 6.2 us)
Async XLA Ops:
  5.1 92.5 %copy-start.3 = (f32[8]{0:T(128)S(1)}, f32[8]{0:T(128)}, u32[]{:S(2)}) copy-start(f32[8]{0:T(128)} %param.10) | copy-start | bytes 100
  5.1 317.3 %copy-start.1 = (s32[4,16,1024]{2,1,0:T(8,128)S(1)}, s32[4,16,1024]{2,1,0:T(8,128)}, u32[]{:S(2)}) copy-start(s32[4,16,1024]{2,1,0:T(8,128)} %param.7) | copy-start | bytes 786436
  5.1 393.3 %copy-start.2 = (s32[4,16,1024]{2,1,0:T(8,128)S(1)}, s32[4,16,1024]{2,1,0:T(8,128)}, u32[]{:S(2)}) copy-start(s32[4,16,1024]{2,1,0:T(8,128)} %param.8) | copy-start | bytes 786436
  5.1 468.1 %copy-start = (bf16[8,4,16,1024]{3,2,1,0:T(8,128)(2,1)S(1)}, bf16[8,4,16,1024]{3,2,1,0:T(8,128)(2,1)}, u32[]{:S(2)}) copy-start(bf16[8,4,16,1024]{3,2,1,0:T(8,128)(2,1)} %param.9) | copy-start | bytes 3145732
  475.7 4.8 collective-permute-start
  478.3 5.7 collective-permute-start.1
  484.2 5.9 %collective-permute-start.2 = (bf16[8,4,20,2]{3,2,1,0:T(8,128)(2,1)S(1)}, bf16[8,4,20,2]{3,2,1,0:T(8,128)(2,1)S(1)}, u32[]{:S(2)}, u32[]{:S(2)}) collective-permute-start(bf16[8,4,20,2]{3,2,1,0:T(8,128)(2,1)S(1)} %get-tuple-element.135), channel_id=1, source_target_pairs={{0,1},{1,2},{2,3},{3,4},{4,5},{5,6},{6,7},{8,9},{9,10},{10,11},{11... | collective-permute-start | bytes 7688 | tf_op jit(solution)/shard_map/ppermute | solution.py:24
  487.5 7.0 %collective-permute-start.3 = (bf16[8,4,20,2]{3,2,1,0:T(8,128)(2,1)S(1)}, bf16[8,4,20,2]{3,2,1,0:T(8,128)(2,1)S(1)}, u32[]{:S(2)}, u32[]{:S(2)}) collective-permute-start(bf16[8,4,20,2]{3,2,1,0:T(8,128)(2,1)S(1)} %get-tuple-element.136), channel_id=1, source_target_pairs={{1,0},{2,1},{3,2},{4,3},{5,4},{6,5},{7,6},{9,8},{10,9},{11,10},{12... | collective-permute-start | bytes 7688 | tf_op jit(solution)/shard_map/ppermute | solution.py:25
  509.6 5.6 collective-permute-start.4
  513.3 6.7 %collective-permute-start.5 = (bf16[8,4,2,1024]{3,2,1,0:T(2,128)(2,1)S(1)}, bf16[8,4,2,1024]{3,2,1,0:T(2,128)(2,1)S(1)}, u32[]{:S(2)}, u32[]{:S(2)}) collective-permute-start(bf16[8,4,2,1024]{3,2,1,0:T(2,128)(2,1)S(1)} %get-tuple-element.140), channel_id=1, source_target_pairs={{8,0},{16,8},{24,16},{32,24},{40,32},{48,40},{56,48},{64,56},{72,6... | collective-permute-start | bytes 393224 | tf_op jit(solution)/shard_map/ppermute | solution.py:25
  520.2 6.5 %collective-permute-start.6 = (bf16[8,4,20,2]{3,2,1,0:T(8,128)(2,1)S(1)}, bf16[8,4,20,2]{3,2,1,0:T(8,128)(2,1)S(1)}, u32[]{:S(2)}, u32[]{:S(2)}) collective-permute-start(bf16[8,4,20,2]{3,2,1,0:T(8,128)(2,1)S(1)} %get-tuple-element.131), channel_id=1, source_target_pairs={{0,1},{1,2},{2,3},{3,4},{4,5},{5,6},{6,7},{8,9},{9,10},{10,11},{11... | collective-permute-start | bytes 7688 | tf_op jit(solution)/shard_map/ppermute | solution.py:24
  524.2 7.0 %collective-permute-start.7 = (bf16[8,4,20,2]{3,2,1,0:T(8,128)(2,1)S(1)}, bf16[8,4,20,2]{3,2,1,0:T(8,128)(2,1)S(1)}, u32[]{:S(2)}, u32[]{:S(2)}) collective-permute-start(bf16[8,4,20,2]{3,2,1,0:T(8,128)(2,1)S(1)} %get-tuple-element.132), channel_id=1, source_target_pairs={{1,0},{2,1},{3,2},{4,3},{5,4},{6,5},{7,6},{9,8},{10,9},{11,10},{12... | collective-permute-start | bytes 7688 | tf_op jit(solution)/shard_map/ppermute | solution.py:25
  546.3 7.4 %collective-permute-start.8 = (bf16[8,4,2,1024]{3,2,1,0:T(2,128)(2,1)S(1)}, bf16[8,4,2,1024]{3,2,1,0:T(2,128)(2,1)S(1)}, u32[]{:S(2)}, u32[]{:S(2)}) collective-permute-start(bf16[8,4,2,1024]{3,2,1,0:T(2,128)(2,1)S(1)} %get-tuple-element.137), channel_id=1, source_target_pairs={{0,8},{8,16},{16,24},{24,32},{32,40},{40,48},{48,56},{56,64},{64,7... | collective-permute-start | bytes 393224 | tf_op jit(solution)/shard_map/ppermute | solution.py:24
  551.8 5.7 collective-permute-start.9
  557.7 5.8 %collective-permute-start.10 = (bf16[8,4,20,2]{3,2,1,0:T(8,128)(2,1)S(1)}, bf16[8,4,20,2]{3,2,1,0:T(8,128)(2,1)S(1)}, u32[]{:S(2)}, u32[]{:S(2)}) collective-permute-start(bf16[8,4,20,2]{3,2,1,0:T(8,128)(2,1)S(1)} %get-tuple-element.127), channel_id=1, source_target_pairs={{0,1},{1,2},{2,3},{3,4},{4,5},{5,6},{6,7},{8,9},{9,10},{10,11},{11... | collective-permute-start | bytes 7688 | tf_op jit(solution)/shard_map/ppermute | solution.py:24
  561.0 7.0 %collective-permute-start.11 = (bf16[8,4,20,2]{3,2,1,0:T(8,128)(2,1)S(1)}, bf16[8,4,20,2]{3,2,1,0:T(8,128)(2,1)S(1)}, u32[]{:S(2)}, u32[]{:S(2)}) collective-permute-start(bf16[8,4,20,2]{3,2,1,0:T(8,128)(2,1)S(1)} %get-tuple-element.128), channel_id=1, source_target_pairs={{1,0},{2,1},{3,2},{4,3},{5,4},{6,5},{7,6},{9,8},{10,9},{11,10},{12... | collective-permute-start | bytes 7688 | tf_op jit(solution)/shard_map/ppermute | solution.py:25
where the time goes:
time: 588 us; the launch traced here: 584 us
  blocking collectives  449 us (76%)
  other arithmetic  61.4 us (10%)
  starting transfers between devices  32.3 us (5%)
  waiting for transfers between devices  27.2 us (5%)
  matrix products  6.88 us (1%)
    psum x5, blocking collectives, per_device(): sums = lax.psum(moments(share, centers, mean, var, weight), ('gy', 'gx'))  367 us
    unnamed x1, blocking collectives  81.5 us
    reduce_max x3, other arithmetic, per_device(): q = jax.nn.softmax(unary + BETA * field, axis=0).astype(jnp.bfloat16)  33.8 us
    ppermute x6, waiting for transfers between devices, extended(): after = lax.ppermute(initial, axis, down)  25.3 us
    ppermute x6, starting transfers between devices, extended(): before = lax.ppermute(last, axis, up)  22.2 us
  transfers between devices with their start and end apart: 12, of which 10 were waited for; matrix products, arithmetic and copies ran while one was open for 0% of the time, Pallas kernels for 0%

commit v1 on v0

--- a/solution.py
+++ b/solution.py
@@ -104,12 +104,13 @@
     mean = init_mean
     var = init_scale * init_scale
     weight = jnp.full((phases,), 1.0 / phases, jnp.float32)
-    share = lax.psum_scatter(counts, ("gy", "gx"), scatter_dimension=0, tiled=True)
-    start = lax.axis_index(("gy", "gx")) * share.shape[0]
-    density = share * scale_factor
-    centers = ((start + jnp.arange(share.shape[0], dtype=jnp.int32)).astype(jnp.float32) + 0.5) / NB
+    counts = lax.psum(counts, ("gy", "gx"))
+    part = NB // devices_all
+    start = lax.axis_index(("gy", "gx")) * part
+    density = lax.dynamic_slice_in_dim(counts, start, part) * scale_factor
+    centers = (jnp.arange(NB, dtype=jnp.int32).astype(jnp.float32) + 0.5) / NB
     for step in range(EM_ITERS):
-        sums = lax.psum(moments(share, centers, mean, var, weight), ("gy", "gx"))
+        sums = moments(counts, centers, mean, var, weight)
         mean, var, weight = refit(sums, float(phases))
     params = jnp.stack([mean, var, weight])
     intensity = (bins.astype(jnp.float32) + 0.5) / NB

time: 588 us -> 220 us (0.37)
  blocking collectives: 449 us -> 81.5 us
    psum x5 -> x1, blocking collectives: 367 us -> 81.5 us  [per_device(): counts = lax.psum(counts, ('gy', 'gx'))]
    unnamed x1 -> x0, blocking collectives: 81.5 us -> none
  transfers between devices with their start and end apart: 12 -> 12, of which waited for: 10 -> 10; matrix products, arithmetic and copies ran while one was open for 0% -> 2% of each run, Pallas kernels for 0% -> 0%
where the time goes in v1:
time: 220 us; the launch traced here: 216 us
  blocking collectives  81.5 us (37%)
  other arithmetic  65.5 us (30%)
  starting transfers between devices  29.5 us (13%)
  waiting for transfers between devices  24.8 us (11%)
  matrix products  6.9 us (3%)
  between operations  4.28 us (2%)
  local copies, waits for them, and re-layouts  2.99 us (1%)
    psum x1, blocking collectives, per_device(): counts = lax.psum(counts, ('gy', 'gx'))  81.5 us
    reduce_max x3, other arithmetic, per_device(): q = jax.nn.softmax(unary + BETA * field, axis=0).astype(jnp.bfloat16)  33.8 us
    ppermute x6, waiting for transfers between devices, extended(): after = lax.ppermute(initial, axis, down)  23 us
    ppermute x6, starting transfers between devices, extended(): before = lax.ppermute(last, axis, up)  19.5 us
    ppermute x6, starting transfers between devices, extended(): after = lax.ppermute(initial, axis, down)  10 us
    concatenate x3, other arithmetic, extended(): x = jnp.concatenate([before, x, after], axis=dim)  8.55 us
    dot_general x4, matrix products, count_block(): lax.dot_general(high_hot, low_hot, (((1,), (1,)), ((), ())), preferred_el...  6.9 us
  transfers between devices with their start and end apart: 12, of which 10 were waited for; matrix products, arithmetic and copies ran while one was open for 2% of the time, Pallas kernels for 0%

profile of v1, /device:TPU:1, one launch (start us, length us, event | category | flops | bytes accessed | tf_op | source)
XLA Modules:
  0.0 215.7 jit_solution(18043125121713261522)
XLA Ops:
  0.7 0.7 multiply_subtract_fusion.5
  1.3 0.8 fusion.37
  2.1 0.8 fusion.28
  2.9 1.0 add_multiply_fusion
  3.9 1.0 convert_element_type.320
  4.9 1.1 copy.9
  6.0 1.1 copy.8
  7.1 10.4 %while.13 = (s32[]{:T(128)}, f32[32,128]{1,0:T(8,128)S(1)}, s32[4,16384]{1,0:T(4,128)S(1)}, s32[4,16384]{1,0:T(4,128)S(1)}, s32[]{:T(128)}, /*index=5*/s32[]{:T(128)}) while((s32[]{:T(128)}, f32[32,128]{1,0:T(8,128)S(1)}, s32[4,16384]{1,0:T(4,128)S(1)}, s32[4,16384]{1,0:T(4,128)S(1)}, s32[]{:T(128)}, /*index=5*/s32[]{:T(128)}) %tuple.82), condition=%wide.region_3.4_spmd.clone, body=%wide.region_2.3_spmd.clone.sunk | while | flops 137715712 | bytes 2719839 | solution.py:100
  7.4 0.3 and_select_fusion.4
  8.0 1.7 fusion.91
  10.0 0.3 and_select_fusion.4
  10.6 1.7 fusion.91
  12.6 0.3 and_select_fusion.4
  13.2 1.7 fusion.91
  15.2 0.3 and_select_fusion.4
  15.8 1.7 fusion.91
  17.5 81.5 %psum.7 = f32[4096]{0:T(1024)S(1)} all-reduce(f32[4096]{0:T(1024)S(1)} %bitcast.43), channel_id=1, replica_groups=mesh['gy'=32,'gx'=8] {'gy','gx'}, use_global_device_ids=true, to_apply=%region_4.5 | all-reduce | flops 4096 | bytes 32768 | tf_op jit(solution)/shard_map/psum | solution.py:107
  99.0 0.8 fusion.38
  100.8 0.8 fusion.40
  102.5 0.8 fusion.42
  104.2 0.8 fusion.44
  106.0 0.8 fusion.46
  107.5 0.6 fusion.61
  108.0 0.7 fusion.18
  108.8 0.9 multiply_convert_fusion.3
  109.9 1.3 collective-permute-start
  111.2 1.3 collective-permute-start.1
  112.5 0.9 collective-permute-done
  113.4 3.5 %collective-permute-done.1 = bf16[8,4,2,1024]{3,2,1,0:T(2,128)(2,1)S(1)} collective-permute-done((bf16[8,4,2,1024]{3,2,1,0:T(2,128)(2,1)S(1)}, bf16[8,4,2,1024]{3,2,1,0:T(2,128)(2,1)S(1)}, u32[]{:S(2)}, u32[]{:S(2)}) %collective-permute-start.1) | collective-permute-done | bytes 131104 | tf_op jit(solution)/shard_map/ppermute | solution.py:25
  116.9 0.9 pad_maximum_fusion.17
  117.8 4.4 %collective-permute-start.2 = (bf16[8,4,20,2]{3,2,1,0:T(8,128)(2,1)}, bf16[8,4,20,2]{3,2,1,0:T(8,128)(2,1)S(1)}, u32[]{:S(2)}, u32[]{:S(2)}) collective-permute-start(bf16[8,4,20,2]{3,2,1,0:T(8,128)(2,1)} %get-tuple-element.136), channel_id=1, source_target_pairs={{0,1},{1,2},{2,3},{3,4},{4,5},{5,6},{6,7},{8,9},{9,10},{10,11},{11... | collective-permute-start | bytes 7688 | tf_op jit(solution)/shard_map/ppermute | solution.py:24
  122.3 2.1 collective-permute-start.3
  124.4 2.1 pad_convert_fusion.2
  126.4 2.8 %collective-permute-done.3 = bf16[8,4,20,2]{3,2,1,0:T(8,128)(2,1)S(1)} collective-permute-done((bf16[8,4,20,2]{3,2,1,0:T(8,128)(2,1)S(1)}, bf16[8,4,20,2]{3,2,1,0:T(8,128)(2,1)S(1)}, u32[]{:S(2)}, u32[]{:S(2)}) %collective-permute-start.3) | collective-permute-done | bytes 2592 | tf_op jit(solution)/shard_map/ppermute | solution.py:25
  129.2 2.8 %maximum_maximum_fusion = (bf16[8,4,20,1026]{3,2,1,0:T(8,128)(2,1)S(1)}, bf16[8,4,20,1026]{3,2,1,0:T(8,128)(2,1)S(1)}) fusion(bf16[8,4,2,1024]{3,2,1,0:T(2,128)(2,1)S(1)} %collective-permute-done.1, bf16[8,4,16,1024]{3,2,1,0:T(8,128)(2,1)S(1)} %multiply_convert_fusion.3, bf16[8,4,2,1024]{3,2,1,0:T(2,128)(2,1)S(1)} %collective-permute-done, ...), kind=kLoop, calls=%fused_computation.45 | loop fusion | flops 10506240 | bytes 3942400 | tf_op jit(solution)/shard_map/concatenate | solution.py:26
  132.1 11.2 %fusion.66 = (f32[4,16,1024]{2,1,0:T(8,128)S(1)}, f32[8,4,16,1024]{3,2,1,0:T(8,128)S(1)}) fusion(f32[8,6,16,1024]{3,2,1,0:T(8,128)S(1)} %copy-done.1, bf16[8,4,20,1026]{3,2,1,0:T(8,128)(2,1)S(1)} %get-tuple-element.135, bf16[8,4,2,1024]{3,2,1,0:T(2,128)(2,1)S(1)} %collective-permute-done.1, bf16[8,4,16,1024]{3,2,1,0:T(8,128)(2,1)S(1)} %multiply_convert_fusion.3, ...), kind=kLoop, calls=%fused_computation.178 | loop fusion | flops 47120384 | bytes 30146656 | tf_op jit(solution)/shard_map/reduce_max | solution.py:124
  143.3 0.3 fusion.19
  143.6 0.4 multiply_convert_fusion.2
  144.3 2.8 %collective-permute-start.4 = (bf16[8,4,2,1024]{3,2,1,0:T(2,128)(2,1)S(1)}, bf16[8,4,2,1024]{3,2,1,0:T(2,128)(2,1)S(1)}, u32[]{:S(2)}, u32[]{:S(2)}) collective-permute-start(bf16[8,4,2,1024]{3,2,1,0:T(2,128)(2,1)S(1)} %get-tuple-element.140), channel_id=1, source_target_pairs={{0,8},{8,16},{16,24},{24,32},{32,40},{40,48},{48,56},{56,64},{64,7... | collective-permute-start | bytes 393224 | tf_op jit(solution)/shard_map/ppermute | solution.py:24
  147.2 1.3 collective-permute-start.5
  148.5 0.6 collective-permute-done.4
  149.1 4.1 %collective-permute-done.5 = bf16[8,4,2,1024]{3,2,1,0:T(2,128)(2,1)S(1)} collective-permute-done((bf16[8,4,2,1024]{3,2,1,0:T(2,128)(2,1)S(1)}, bf16[8,4,2,1024]{3,2,1,0:T(2,128)(2,1)S(1)}, u32[]{:S(2)}, u32[]{:S(2)}) %collective-permute-start.5) | collective-permute-done | bytes 131104 | tf_op jit(solution)/shard_map/ppermute | solution.py:25
  153.4 4.0 %collective-permute-start.6 = (bf16[8,4,20,2]{3,2,1,0:T(8,128)(2,1)S(1)}, bf16[8,4,20,2]{3,2,1,0:T(8,128)(2,1)S(1)}, u32[]{:S(2)}, u32[]{:S(2)}) collective-permute-start(bf16[8,4,20,2]{3,2,1,0:T(8,128)(2,1)S(1)} %get-tuple-element.132), channel_id=1, source_target_pairs={{0,1},{1,2},{2,3},{3,4},{4,5},{5,6},{6,7},{8,9},{9,10},{10,11},{11... | collective-permute-start | bytes 7688 | tf_op jit(solution)/shard_map/ppermute | solution.py:24
  157.4 1.9 collective-permute-start.7
  159.3 0.4 pad_convert_fusion.1
  159.7 0.3 collective-permute-done.6
  160.0 4.4 %collective-permute-done.7 = bf16[8,4,20,2]{3,2,1,0:T(8,128)(2,1)S(1)} collective-permute-done((bf16[8,4,20,2]{3,2,1,0:T(8,128)(2,1)S(1)}, bf16[8,4,20,2]{3,2,1,0:T(8,128)(2,1)S(1)}, u32[]{:S(2)}, u32[]{:S(2)}) %collective-permute-start.7) | collective-permute-done | bytes 2592 | tf_op jit(solution)/shard_map/ppermute | solution.py:25
  164.4 2.9 %maximum_maximum_fusion.1 = (bf16[8,4,20,1026]{3,2,1,0:T(8,128)(2,1)S(1)}, bf16[8,4,20,1026]{3,2,1,0:T(8,128)(2,1)S(1)}) fusion(bf16[8,4,2,1024]{3,2,1,0:T(2,128)(2,1)S(1)} %collective-permute-done.5, bf16[8,4,16,1024]{3,2,1,0:T(8,128)(2,1)S(1)} %multiply_convert_fusion.2, bf16[8,4,2,1024]{3,2,1,0:T(2,128)(2,1)S(1)} %collective-permute-done.4, ...), kind=kLoop, calls=%fused_computation.47 | loop fusion | flops 10506240 | bytes 3942400 | tf_op jit(solution)/shard_map/concatenate | solution.py:26
  167.2 11.3 %fusion.64 = (f32[4,16,1024]{2,1,0:T(8,128)S(1)}, f32[8,4,16,1024]{3,2,1,0:T(8,128)S(1)}) fusion(f32[8,6,16,1024]{3,2,1,0:T(8,128)S(1)} %pad_convert_fusion.1, bf16[8,4,20,1026]{3,2,1,0:T(8,128)(2,1)S(1)} %get-tuple-element.131, bf16[8,4,2,1024]{3,2,1,0:T(2,128)(2,1)S(1)} %collective-permute-done.5, bf16[8,4,16,1024]{3,2,1,0:T(8,128)(2,1)S(1)} %multiply_convert_fusion.2, ...), kind=kLoop, calls=%fused_computation.177 | loop fusion | flops 47120384 | bytes 30146656 | tf_op jit(solution)/shard_map/reduce_max | solution.py:124
  178.5 0.3 fusion.20
  178.8 0.4 multiply_convert_fusion.1
  179.5 4.0 %collective-permute-start.8 = (bf16[8,4,2,1024]{3,2,1,0:T(2,128)(2,1)S(1)}, bf16[8,4,2,1024]{3,2,1,0:T(2,128)(2,1)S(1)}, u32[]{:S(2)}, u32[]{:S(2)}) collective-permute-start(bf16[8,4,2,1024]{3,2,1,0:T(2,128)(2,1)S(1)} %get-tuple-element.138), channel_id=1, source_target_pairs={{0,8},{8,16},{16,24},{24,32},{32,40},{40,48},{48,56},{56,64},{64,7... | collective-permute-start | bytes 393224 | tf_op jit(solution)/shard_map/ppermute | solution.py:24
  183.5 1.3 collective-permute-start.9
  184.8 0.6 dynamic-slice_multiply_fusion
  185.4 0.6 pad_maximum_fusion.18
  186.0 3.8 %collective-permute-done.9 = bf16[8,4,2,1024]{3,2,1,0:T(2,128)(2,1)S(1)} collective-permute-done((bf16[8,4,2,1024]{3,2,1,0:T(2,128)(2,1)S(1)}, bf16[8,4,2,1024]{3,2,1,0:T(2,128)(2,1)S(1)}, u32[]{:S(2)}, u32[]{:S(2)}) %collective-permute-start.9) | collective-permute-done | bytes 131104 | tf_op jit(solution)/shard_map/ppermute | solution.py:25
  190.0 2.9 %collective-permute-start.10 = (bf16[8,4,20,2]{3,2,1,0:T(8,128)(2,1)S(1)}, bf16[8,4,20,2]{3,2,1,0:T(8,128)(2,1)S(1)}, u32[]{:S(2)}, u32[]{:S(2)}) collective-permute-start(bf16[8,4,20,2]{3,2,1,0:T(8,128)(2,1)S(1)} %get-tuple-element.128), channel_id=1, source_target_pairs={{0,1},{1,2},{2,3},{3,4},{4,5},{5,6},{6,7},{8,9},{9,10},{10,11},{11... | collective-permute-start | bytes 7688 | tf_op jit(solution)/shard_map/ppermute | solution.py:24
  192.9 2.1 collective-permute-start.11
  195.1 0.4 pad_convert_fusion
  195.5 4.4 %collective-permute-done.11 = bf16[8,4,20,2]{3,2,1,0:T(8,128)(2,1)S(1)} collective-permute-done((bf16[8,4,20,2]{3,2,1,0:T(8,128)(2,1)S(1)}, bf16[8,4,20,2]{3,2,1,0:T(8,128)(2,1)S(1)}, u32[]{:S(2)}, u32[]{:S(2)}) %collective-permute-start.11) | collective-permute-done | bytes 2592 | tf_op jit(solution)/shard_map/ppermute | solution.py:25
  199.9 2.9 %maximum_maximum_fusion.2 = (bf16[8,4,20,1026]{3,2,1,0:T(8,128)(2,1)S(1)}, bf16[8,4,20,1026]{3,2,1,0:T(8,128)(2,1)S(1)}) fusion(bf16[8,4,2,1024]{3,2,1,0:T(2,128)(2,1)S(1)} %collective-permute-done.9, bf16[8,4,16,1024]{3,2,1,0:T(8,128)(2,1)S(1)} %multiply_convert_fusion.1, bf16[8,4,2,1024]{3,2,1,0:T(2,128)(2,1)S(1)} %collective-permute-done.8, ...), kind=kLoop, calls=%fused_computation.49 | loop fusion | flops 10506240 | bytes 3942400 | tf_op jit(solution)/shard_map/concatenate | solution.py:26
  202.8 11.3 %fusion.62 = (f32[4,16,1024]{2,1,0:T(8,128)S(1)}, f32[8,4,16,1024]{3,2,1,0:T(8,128)S(1)}) fusion(f32[8,6,16,1024]{3,2,1,0:T(8,128)S(1)} %pad_convert_fusion, bf16[8,4,20,1026]{3,2,1,0:T(8,128)(2,1)S(1)} %get-tuple-element.127, bf16[8,4,2,1024]{3,2,1,0:T(2,128)(2,1)S(1)} %collective-permute-done.9, bf16[8,4,16,1024]{3,2,1,0:T(8,128)(2,1)S(1)} %multiply_convert_fusion.1, ...), kind=kLoop, calls=%fused_computation.176 | loop fusion | flops 47120384 | bytes 30146656 | tf_op jit(solution)/shard_map/reduce_max | solution.py:124
  214.0 0.3 fusion.21
  214.3 1.4 multiply_convert_fusion
  (47 shorter events, 4.4 us)
Async XLA Ops:
  7.1 91.9 %copy-start.2 = (f32[8]{0:T(128)S(1)}, f32[8]{0:T(128)}, u32[]{:S(2)}) copy-start(f32[8]{0:T(128)} %param.10) | copy-start | bytes 100
  7.1 100.3 %copy-start = (bf16[8,4,16,1024]{3,2,1,0:T(8,128)(2,1)S(1)}, bf16[8,4,16,1024]{3,2,1,0:T(8,128)(2,1)}, u32[]{:S(2)}) copy-start(bf16[8,4,16,1024]{3,2,1,0:T(8,128)(2,1)} %param.9) | copy-start | bytes 3145732
  109.9 3.5 %collective-permute-start = (bf16[8,4,2,1024]{3,2,1,0:T(2,128)(2,1)S(1)}, bf16[8,4,2,1024]{3,2,1,0:T(2,128)(2,1)S(1)}, u32[]{:S(2)}, u32[]{:S(2)}) collective-permute-start(bf16[8,4,2,1024]{3,2,1,0:T(2,128)(2,1)S(1)} %get-tuple-element.142), channel_id=1, source_target_pairs={{0,8},{8,16},{16,24},{24,32},{32,40},{40,48},{48,56},{56,64},{64,7... | collective-permute-start | bytes 393224 | tf_op jit(solution)/shard_map/ppermute | solution.py:24
  111.2 5.7 %collective-permute-start.1 = (bf16[8,4,2,1024]{3,2,1,0:T(2,128)(2,1)S(1)}, bf16[8,4,2,1024]{3,2,1,0:T(2,128)(2,1)S(1)}, u32[]{:S(2)}, u32[]{:S(2)}) collective-permute-start(bf16[8,4,2,1024]{3,2,1,0:T(2,128)(2,1)S(1)} %get-tuple-element.143), channel_id=1, source_target_pairs={{8,0},{16,8},{24,16},{32,24},{40,32},{48,40},{56,48},{64,56},{72,6... | collective-permute-start | bytes 393224 | tf_op jit(solution)/shard_map/ppermute | solution.py:25
  117.8 8.6 %collective-permute-start.2 = (bf16[8,4,20,2]{3,2,1,0:T(8,128)(2,1)}, bf16[8,4,20,2]{3,2,1,0:T(8,128)(2,1)S(1)}, u32[]{:S(2)}, u32[]{:S(2)}) collective-permute-start(bf16[8,4,20,2]{3,2,1,0:T(8,128)(2,1)} %get-tuple-element.136), channel_id=1, source_target_pairs={{0,1},{1,2},{2,3},{3,4},{4,5},{5,6},{6,7},{8,9},{9,10},{10,11},{11... | collective-permute-start | bytes 7688 | tf_op jit(solution)/shard_map/ppermute | solution.py:24
  122.3 7.0 %collective-permute-start.3 = (bf16[8,4,20,2]{3,2,1,0:T(8,128)(2,1)S(1)}, bf16[8,4,20,2]{3,2,1,0:T(8,128)(2,1)S(1)}, u32[]{:S(2)}, u32[]{:S(2)}) collective-permute-start(bf16[8,4,20,2]{3,2,1,0:T(8,128)(2,1)S(1)} %get-tuple-element.137), channel_id=1, source_target_pairs={{1,0},{2,1},{3,2},{4,3},{5,4},{6,5},{7,6},{9,8},{10,9},{11,10},{12... | collective-permute-start | bytes 7688 | tf_op jit(solution)/shard_map/ppermute | solution.py:25
  126.4 5.7 %copy-start.1 = (f32[8,6,16,1024]{3,2,1,0:T(8,128)S(1)}, f32[8,6,16,1024]{3,2,1,0:T(8,128)}, u32[]{:S(2)}) copy-start(f32[8,6,16,1024]{3,2,1,0:T(8,128)} %pad_convert_fusion.2) | copy-start | bytes 9437188
  144.3 4.8 %collective-permute-start.4 = (bf16[8,4,2,1024]{3,2,1,0:T(2,128)(2,1)S(1)}, bf16[8,4,2,1024]{3,2,1,0:T(2,128)(2,1)S(1)}, u32[]{:S(2)}, u32[]{:S(2)}) collective-permute-start(bf16[8,4,2,1024]{3,2,1,0:T(2,128)(2,1)S(1)} %get-tuple-element.140), channel_id=1, source_target_pairs={{0,8},{8,16},{16,24},{24,32},{32,40},{40,48},{48,56},{56,64},{64,7... | collective-permute-start | bytes 393224 | tf_op jit(solution)/shard_map/ppermute | solution.py:24
  147.2 6.0 %collective-permute-start.5 = (bf16[8,4,2,1024]{3,2,1,0:T(2,128)(2,1)S(1)}, bf16[8,4,2,1024]{3,2,1,0:T(2,128)(2,1)S(1)}, u32[]{:S(2)}, u32[]{:S(2)}) collective-permute-start(bf16[8,4,2,1024]{3,2,1,0:T(2,128)(2,1)S(1)} %get-tuple-element.141), channel_id=1, source_target_pairs={{8,0},{16,8},{24,16},{32,24},{40,32},{48,40},{56,48},{64,56},{72,6... | collective-permute-start | bytes 393224 | tf_op jit(solution)/shard_map/ppermute | solution.py:25
  153.4 6.6 %collective-permute-start.6 = (bf16[8,4,20,2]{3,2,1,0:T(8,128)(2,1)S(1)}, bf16[8,4,20,2]{3,2,1,0:T(8,128)(2,1)S(1)}, u32[]{:S(2)}, u32[]{:S(2)}) collective-permute-start(bf16[8,4,20,2]{3,2,1,0:T(8,128)(2,1)S(1)} %get-tuple-element.132), channel_id=1, source_target_pairs={{0,1},{1,2},{2,3},{3,4},{4,5},{5,6},{6,7},{8,9},{9,10},{10,11},{11... | collective-permute-start | bytes 7688 | tf_op jit(solution)/shard_map/ppermute | solution.py:24
  157.4 7.0 %collective-permute-start.7 = (bf16[8,4,20,2]{3,2,1,0:T(8,128)(2,1)S(1)}, bf16[8,4,20,2]{3,2,1,0:T(8,128)(2,1)S(1)}, u32[]{:S(2)}, u32[]{:S(2)}) collective-permute-start(bf16[8,4,20,2]{3,2,1,0:T(8,128)(2,1)S(1)} %get-tuple-element.133), channel_id=1, source_target_pairs={{1,0},{2,1},{3,2},{4,3},{5,4},{6,5},{7,6},{9,8},{10,9},{11,10},{12... | collective-permute-start | bytes 7688 | tf_op jit(solution)/shard_map/ppermute | solution.py:25
  179.5 6.5 %collective-permute-start.8 = (bf16[8,4,2,1024]{3,2,1,0:T(2,128)(2,1)S(1)}, bf16[8,4,2,1024]{3,2,1,0:T(2,128)(2,1)S(1)}, u32[]{:S(2)}, u32[]{:S(2)}) collective-permute-start(bf16[8,4,2,1024]{3,2,1,0:T(2,128)(2,1)S(1)} %get-tuple-element.138), channel_id=1, source_target_pairs={{0,8},{8,16},{16,24},{24,32},{32,40},{40,48},{48,56},{56,64},{64,7... | collective-permute-start | bytes 393224 | tf_op jit(solution)/shard_map/ppermute | solution.py:24
  183.5 6.3 %collective-permute-start.9 = (bf16[8,4,2,1024]{3,2,1,0:T(2,128)(2,1)S(1)}, bf16[8,4,2,1024]{3,2,1,0:T(2,128)(2,1)S(1)}, u32[]{:S(2)}, u32[]{:S(2)}) collective-permute-start(bf16[8,4,2,1024]{3,2,1,0:T(2,128)(2,1)S(1)} %get-tuple-element.139), channel_id=1, source_target_pairs={{8,0},{16,8},{24,16},{32,24},{40,32},{48,40},{56,48},{64,56},{72,6... | collective-permute-start | bytes 393224 | tf_op jit(solution)/shard_map/ppermute | solution.py:25
  190.0 5.5 %collective-permute-start.10 = (bf16[8,4,20,2]{3,2,1,0:T(8,128)(2,1)S(1)}, bf16[8,4,20,2]{3,2,1,0:T(8,128)(2,1)S(1)}, u32[]{:S(2)}, u32[]{:S(2)}) collective-permute-start(bf16[8,4,20,2]{3,2,1,0:T(8,128)(2,1)S(1)} %get-tuple-element.128), channel_id=1, source_target_pairs={{0,1},{1,2},{2,3},{3,4},{4,5},{5,6},{6,7},{8,9},{9,10},{10,11},{11... | collective-permute-start | bytes 7688 | tf_op jit(solution)/shard_map/ppermute | solution.py:24
  192.9 7.0 %collective-permute-start.11 = (bf16[8,4,20,2]{3,2,1,0:T(8,128)(2,1)S(1)}, bf16[8,4,20,2]{3,2,1,0:T(8,128)(2,1)S(1)}, u32[]{:S(2)}, u32[]{:S(2)}) collective-permute-start(bf16[8,4,20,2]{3,2,1,0:T(8,128)(2,1)S(1)} %get-tuple-element.129), channel_id=1, source_target_pairs={{1,0},{2,1},{3,2},{4,3},{5,4},{6,5},{7,6},{9,8},{10,9},{11,10},{12... | collective-permute-start | bytes 7688 | tf_op jit(solution)/shard_map/ppermute | solution.py:25

commit v2 on v0

v2 whole, which is shorter than its diff:
```python
import functools
import math

import jax
import jax.numpy as jnp
import numpy as np
from jax import lax
from jax.experimental import pallas as pl
from jax.experimental.pallas import tpu as pltpu
from jax.sharding import PartitionSpec as P

NB = 4096
EM_ITERS = 5
VAR_EPS = 1e-05
BETA = 0.3
LOG2E = math.log2(math.e)
MESH = pl.DeviceIdType.MESH

PH = 8
PL = 4
ROWS = 16
COLS = 1024
STEP = 116
CHUNKS = 9
NX, NY, NZ = 4, 4, 8


def neighbours(gy, gx, ny, nx):
    up, down = lax.rem(gy + ny - 1, ny), lax.rem(gy + 1, ny)
    left, right = lax.rem(gx + nx - 1, nx), lax.rem(gx + 1, nx)
    return up, down, left, right


def front_kernel(
    bins_ref, mask_ref, atlas_ref,
    counts_ref, rows_a, side_a, corner_a, rows_c, side_c, corner_c,
    code, high, low, half, core_in, x_in, y_in, z_in, stage, total,
    halo_send, halo_recv, sum_send, sum_recv,
):
    ny, nx = lax.axis_size("gy"), lax.axis_size("gx")
    gy, gx = lax.axis_index("gy"), lax.axis_index("gx")
    up, down, left, right = neighbours(gy, gx, ny, nx)
    core, x = lax.rem(gx, 2), gx // 2
    y, z = lax.rem(gy, NY), gy // NY
    other = gx + 1 - 2 * core
    along_x = [(gy, lax.rem(x + d, NX) * 2 + core) for d in range(1, NX)]
    along_y = [(z * NY + lax.rem(y + d, NY), gx) for d in range(1, NY)]
    along_z = [(lax.rem(z + d, NZ) * NY + y, gx) for d in range(1, NZ)]
    around = [
        (up, gx), (down, gx), (gy, left), (gy, right),
        (up, left), (up, right), (down, left), (down, right),
    ]
    partners = [(gy, other)] + along_x + along_y + along_z + around

    barrier = pltpu.get_barrier_semaphore()
    for device in partners:
        pl.semaphore_signal(barrier, inc=1, device_id=device, device_id_type=MESH)

    code[...] = bins_ref[...] + NB * mask_ref[...]
    for plane in range(PL):
        b = bins_ref[plane]
        keep = mask_ref[plane] > 0
        high[plane * ROWS : (plane + 1) * ROWS, :] = jnp.where(keep, b // 64, 255).astype(jnp.float32)
        low[plane * ROWS : (plane + 1) * ROWS, :] = (b & 63).astype(jnp.float32)

    pl.semaphore_wait(barrier, len(partners))

    bottom, top = pl.ds(ROWS - 8, 8), pl.ds(0, 8)
    last, first = pl.ds(COLS - 128, 128), pl.ds(0, 128)
    every, wide = pl.ds(0, ROWS), pl.ds(0, COLS)
    plan = [
        ((up, gx), top, wide, rows_a.at[1], rows_c.at[1]),
        ((down, gx), bottom, wide, rows_a.at[0], rows_c.at[0]),
        ((gy, left), every, first, side_a.at[1], side_c.at[1]),
        ((gy, right), every, last, side_a.at[0], side_c.at[0]),
        ((up, left), top, first, corner_a.at[3], corner_c.at[3]),
        ((up, right), top, last, corner_a.at[2], corner_c.at[2]),
        ((down, left), bottom, first, corner_a.at[1], corner_c.at[1]),
        ((down, right), bottom, last, corner_a.at[0], corner_c.at[0]),
    ]
    copies = []
    for n, (device, r, c, to_a, to_c) in enumerate(plan):
        for m, (src, dst) in enumerate(((atlas_ref.at[:, :, r, c], to_a), (code.at[:, r, c], to_c))):
            copies.append(
                pltpu.make_async_remote_copy(
                    src_ref=src, dst_ref=dst,
                    send_sem=halo_send.at[2 * n + m], recv_sem=halo_recv.at[2 * n + m],
                    device_id=device, device_id_type=MESH,
                )
            )
    for copy in copies:
        copy.start()

    levels = lax.broadcasted_iota(jnp.int32, (64, COLS), 0).astype(jnp.float32).astype(jnp.bfloat16)
    one, zero = jnp.ones((), jnp.bfloat16), jnp.zeros((), jnp.bfloat16)
    total[...] = jnp.zeros_like(total)

    def count(r, carry):
        h = jnp.broadcast_to(high[pl.ds(r, 1), :], (64, COLS)).astype(jnp.bfloat16)
        l = jnp.broadcast_to(low[pl.ds(r, 1), :], (64, COLS)).astype(jnp.bfloat16)
        hot_h = jnp.where(h == levels, one, zero)
        hot_l = jnp.where(l == levels, one, zero)
        total[...] += lax.dot_general(
            hot_h, hot_l, (((1,), (1,)), ((), ())), preferred_element_type=jnp.float32
        )
        return carry

    lax.fori_loop(0, PL * ROWS, count, 0)
    mine = total[...]
    half[...] = mine

    def exchange(src, dst, device, n):
        return pltpu.make_async_remote_copy(
            src_ref=src, dst_ref=dst, send_sem=sum_send.at[n], recv_sem=sum_recv.at[n],
            device_id=device, device_id_type=MESH,
        )

    keep_rows = pl.ds(pl.multiple_of(core * 32, 32), 32)
    give_rows = pl.ds(pl.multiple_of((1 - core) * 32, 32), 32)
    done = []
    copy = exchange(half.at[give_rows], core_in, (gy, other), 0)
    copy.start()
    copy.wait_recv()
    done.append(copy)
    stage[0] = half[keep_rows, :] + core_in[...]
    n = 1
    for level, (group, landing) in enumerate(((along_x, x_in), (along_y, y_in), (along_z, z_in))):
        now = []
        for i, device in enumerate(group):
            now.append(exchange(stage.at[level], landing.at[i], device, n))
            n += 1
        for copy in now:
            copy.start()
        acc = stage[level]
        for i, copy in enumerate(now):
            copy.wait_recv()
            acc = acc + landing[i]
        stage[level + 1] = acc
        done += now
    copy = exchange(stage.at[3], counts_ref.at[keep_rows], (gy, other), n)
    copy.start()
    counts_ref[keep_rows, :] = stage[3]
    copy.wait_recv()
    done.append(copy)
    for copy in done:
        copy.wait_send()
    for copy in copies:
        copy.wait()


def front(bins, mask, atlas):
    f32, bf16, i32 = jnp.float32, jnp.bfloat16, jnp.int32
    vmem = pl.BlockSpec(memory_space=pltpu.VMEM)
    anywhere = pl.BlockSpec(memory_space=pl.ANY)
    sds = jax.ShapeDtypeStruct
    sums = 2 + (NX - 1) + (NY - 1) + (NZ - 1)
    return pl.pallas_call(
        front_kernel,
        out_shape=(
            sds((64, 64), f32),
            sds((2, PH, PL, 8, COLS), bf16),
            sds((2, PH, PL, ROWS, 128), bf16),
            sds((4, PH, PL, 8, 128), bf16),
            sds((2, PL, 8, COLS), i32),
            sds((2, PL, ROWS, 128), i32),
            sds((4, PL, 8, 128), i32),
        ),
        in_specs=[vmem, vmem, anywhere],
        out_specs=(vmem,) + (anywhere,) * 6,
        scratch_shapes=[
            pltpu.VMEM((PL, ROWS, COLS), i32),
            pltpu.VMEM((PL * ROWS, COLS), f32),
            pltpu.VMEM((PL * ROWS, COLS), f32),
            pltpu.VMEM((64, 64), f32),
            pltpu.VMEM((32, 64), f32),
            pltpu.VMEM((NX - 1, 32, 64), f32),
            pltpu.VMEM((NY - 1, 32, 64), f32),
            pltpu.VMEM((NZ - 1, 32, 64), f32),
            pltpu.VMEM((4, 32, 64), f32),
            pltpu.VMEM((64, 64), f32),
            pltpu.SemaphoreType.DMA((16,)),
            pltpu.SemaphoreType.DMA((16,)),
            pltpu.SemaphoreType.DMA((sums,)),
            pltpu.SemaphoreType.DMA((sums,)),
        ],
        compiler_params=pltpu.CompilerParams(collective_id=0, has_side_effects=True),
        name="histogram_and_halo",
    )(bins, mask, atlas)


def fit(counts_ref, mean, scale):
    wide = [jnp.broadcast_to(counts_ref[r : r + 1, :], (PH, 128)) for r in range(NB // 128)]
    counts = jnp.concatenate(wide, axis=1)
    centers = (lax.broadcasted_iota(jnp.int32, (PH, NB), 1).astype(jnp.float32) + 0.5) / NB
    first_w = counts * centers
    second_w = first_w * centers
    var = scale * scale
    weight = jnp.full((PH, 1), 1.0 / PH, jnp.float32)
    for step in range(EM_ITERS):
        diff = centers - mean
        scores = (jnp.log(weight) - 0.5 * jnp.log(var)) - diff * diff * (0.5 / var)
        e = jnp.exp(scores - jnp.max(scores, axis=0, keepdims=True))
        resp = e * (1.0 / jnp.sum(e, axis=0, keepdims=True))
        occ = jnp.sum(resp * counts, axis=1, keepdims=True)
        first = jnp.sum(resp * first_w, axis=1, keepdims=True)
        second = jnp.sum(resp * second_w, axis=1, keepdims=True)
        mean = first / (occ + 1.0)
        var = (second - first * mean) / (occ + 1.0) + VAR_EPS
        weight = (occ + 1.0) / (jnp.sum(occ, axis=0, keepdims=True) + float(PH))
    return mean, var, weight


def softmax_into(t, r_mask):
    top = functools.reduce(jnp.maximum, t)
    e = [jnp.exp2(v - top) for v in t]
    inv = jnp.where(r_mask > 0.0, 1.0 / functools.reduce(jnp.add, e), 0.0)
    return [v * inv for v in e]


def back_kernel(
    place_ref, counts_ref, mean_ref, scale_ref, bins_ref, mask_ref, atlas_ref,
    rows_a, side_a, corner_a, rows_c, side_c, corner_c, w_ref,
    prob_ref, params_ref, density_ref,
    apad, cpad, coef, uns, msk, held, held24, pa, pb, pd, ps, kept,
):
    f32, bf16 = jnp.float32, jnp.bfloat16
    gy, gx = place_ref[0], place_ref[1]
    ny, nx = place_ref[2], place_ref[3]

    row = counts_ref[pl.ds(gy, 1), :] * place_scale(bins_ref)
    density_ref[...] = pltpu.roll(jnp.broadcast_to(row, (8, 128)), lax.rem(128 - gx * 16, 128), 1)[0:1, 0:16]
    mean, var, weight = fit(counts_ref, mean_ref[...], scale_ref[...])
    lane = lax.broadcasted_iota(jnp.int32, (PH, 128), 1)
    diag = lane == lax.broadcasted_iota(jnp.int32, (PH, 128), 0)
    for n, column in enumerate((mean, var, weight)):
        spread = jnp.where(diag, jnp.broadcast_to(column, (PH, 128)), 0.0)
        params_ref[n : n + 1, :] = jnp.sum(spread, axis=0, keepdims=True)[:, 0:PH]
    offset = (jnp.log(weight) - 0.5 * jnp.log(var)) * LOG2E
    slope = (0.5 * LOG2E) / var
    for n, column in enumerate((mean, offset, slope)):
        full = jnp.broadcast_to(column, (PH, 128))
        for k in range(PH):
            coef[n, k] = jnp.broadcast_to(full[k : k + 1, :], (8, 128))

    own, over = pl.ds(128, COLS), pl.ds(128 + COLS, 128)

    def fill(k, carry):
        for plane in range(PL):
            apad[k, plane, 8:24, own] = atlas_ref[k, plane]
            apad[k, plane, 8:24, 0:128] = side_a[0, k, plane]
            apad[k, plane, 8:24, over] = side_a[1, k, plane]
            apad[k, plane, 0:8, own] = rows_a[0, k, plane]
            apad[k, plane, 24:32, own] = rows_a[1, k, plane]
            apad[k, plane, 0:8, 0:128] = corner_a[0, k, plane]
            apad[k, plane, 0:8, over] = corner_a[1, k, plane]
            apad[k, plane, 24:32, 0:128] = corner_a[2, k, plane]
            apad[k, plane, 24:32, over] = corner_a[3, k, plane]
        return carry

    lax.fori_loop(0, PH, fill, 0)
    has_up, has_down = gy > 0, gy < ny - 1
    has_left, has_right = gx > 0, gx < nx - 1
    cpad[:, 8:24, own] = bins_ref[...] + NB * mask_ref[...]
    cpad[:, 8:24, 0:128] = jnp.where(has_left, side_c[0], 0)
    cpad[:, 8:24, over] = jnp.where(has_right, side_c[1], 0)
    cpad[:, 0:8, own] = jnp.where(has_up, rows_c[0], 0)
    cpad[:, 24:32, own] = jnp.where(has_down, rows_c[1], 0)
    cpad[:, 0:8, 0:128] = jnp.where(has_up & has_left, corner_c[0], 0)
    cpad[:, 0:8, over] = jnp.where(has_up & has_right, corner_c[1], 0)
    cpad[:, 24:32, 0:128] = jnp.where(has_down & has_left, corner_c[2], 0)
    cpad[:, 24:32, over] = jnp.where(has_down & has_right, corner_c[3], 0)

    held[PL] = jnp.zeros_like(held[PL])
    held24[PL] = jnp.zeros_like(held24[PL])
    ps[0] = jnp.zeros_like(ps[0])
    for ref in (pa, pb, pd):
        for plane in range(PL):
            ref[plane, 0:8] = jnp.zeros((8, 128), f32)
            ref[plane, 200:208] = jnp.zeros((8, 128), f32)
    beta = BETA / 5.0 * LOG2E
    at = lax.broadcasted_iota(jnp.int32, (8, 128), 1)

    def spread_sums(src, per, lead):
        def plane_dot(plane, carry):
            both = jnp.concatenate([src[plane], src[plane + 1]], axis=1)
            out = jnp.dot(both, w_ref[...], preferred_element_type=f32)
            span = pl.ds(lead, per)
            pa[plane, span, :] = out[:, 0:128]
            pb[plane, span, :] = out[:, 128:256]
            pd[plane, span, :] = out[:, 256:384]
            ps[plane + 1, span, :] = out[:, 384:512]
            return carry

        lax.fori_loop(0, PL, plane_dot, 0)

    def update(plane, start, u_start, m_start, per):
        t = []
        for k in range(PH):
            r = k * per + start
            total = pa[plane, pl.ds(r, 8), :] + ps[plane, pl.ds(r, 8), :]
            total = total + (pb[plane, pl.ds(r - 1, 8), :] + pb[plane, pl.ds(r + 1, 8), :])
            total = total + (pd[plane, pl.ds(r - 2, 8), :] + pd[plane, pl.ds(r + 2, 8), :])
            t.append(uns[plane, pl.ds(k * 32 + u_start, 8), :] + beta * total)
        return softmax_into(t, msk[plane, pl.ds(m_start, 8), :])

    def chunk(c, carry):
        turn = 12 * c + 6
        from_right = at < 128 - turn - 0

        def moved(a, b):
            return pltpu.roll(jnp.where(from_right, b, a), turn, 1)

        tile_a = pl.ds(pl.multiple_of(c * 128, 128), 128)
        tile_b = pl.ds(pl.multiple_of((c + 1) * 128, 128), 128)

        def begin(plane, carry):
            for pair in range(2):
                outs = []
                rows16 = pl.ds(pair * 16, 16)
                left = [apad[k, plane, rows16, tile_a].astype(f32) for k in range(PH)]
                right = [apad[k, plane, rows16, tile_b].astype(f32) for k in range(PH)]
                for sub in range(2):
                    g = pair * 16 + sub * 8
                    s8 = slice(sub * 8, sub * 8 + 8)
                    cd = moved(cpad[plane, pl.ds(g, 8), tile_a], cpad[plane, pl.ds(g, 8), tile_b])
                    keep = cd >= NB
                    m = jnp.where(keep, 1.0, 0.0)
                    msk[plane, pl.ds(g, 8), :] = m
                    s = ((cd & (NB - 1)).astype(f32) + 0.5) * (1.0 / NB)
                    t = []
                    for k in range(PH):
                        prior = moved(left[k][s8], right[k][s8])
                        d = s - coef[0, k]
                        u = (coef[1, k] - d * d * coef[2, k]) + prior * LOG2E
                        u = jnp.where(keep, u, 0.0)
                        uns[plane, pl.ds(k * 32 + g, 8), :] = u
                        t.append(u)
                    outs.append(softmax_into(t, m))
                for k in range(PH):
                    both = jnp.concatenate([outs[0][k], outs[1][k]], axis=0)
                    held[plane, pl.ds(k * 32 + pair * 16, 16), :] = both.astype(bf16)
            return carry

        lax.fori_loop(0, PL, begin, 0)

        def store24(plane, outs):
            flat = [outs[i][k] for k in range(PH) for i in range(3)]
            for f in range(0, 3 * PH, 2):
                both = jnp.concatenate([flat[f], flat[f + 1]], axis=0)
                held24[plane, pl.ds(f * 8, 16), :] = both.astype(bf16)

        spread_sums(held, 256, 0)

        def second(plane, carry):
            store24(plane, [update(plane, 4 + 8 * i, 4 + 8 * i, 4 + 8 * i, 32) for i in range(3)])
            return carry

        lax.fori_loop(0, PL, second, 0)
        spread_sums(held24, 192, 8)

        def third(plane, carry):
            store24(plane, [update(plane, 8 + 8 * i, 4 + 8 * i, 4 + 8 * i, 24) for i in range(3)])
            return carry

        lax.fori_loop(0, PL, third, 0)
        spread_sums(held24, 192, 8)
        slot = lax.rem(c, 2)
        before = at < STEP + 12 - 12 * c
        tile_out = pl.ds(pl.multiple_of(jnp.maximum(c - 1, 0) * 128, 128), 128)

        def last(plane, carry):
            outs = [update(plane, 8 + 4 + 8 * i, 8 + 8 * i, 8 + 8 * i, 24) for i in range(2)]
            for k in range(PH):
                full = []
                for i in range(2):
                    v = pltpu.roll(outs[i][k], 128 - turn, 1)
                    old = kept[1 - slot, plane, k, pl.ds(8 * i, 8), :]
                    kept[slot, plane, k, pl.ds(8 * i, 8), :] = v
                    full.append(jnp.where(before, old, v))
                prob_ref[k, plane, :, tile_out] = jnp.concatenate(full, axis=0).astype(bf16)
            return carry

        lax.fori_loop(0, PL, last, 0)
        return carry

    lax.fori_loop(0, CHUNKS, chunk, 0)


def place_scale(bins_ref):
    planes, rows, cols = bins_ref.shape
    return float(NB) / float(planes * rows * cols * 2 * NX * NY * NZ)


def stencil_weights():
    i = np.arange(128)
    d = np.abs(i[:, None] - i[None, :])

    def band(*values):
        out = np.zeros((128, 128), np.float32)
        for n, v in enumerate(values):
            out[d == n] = v
        return out

    eye, none = band(5.0), np.zeros((128, 128), np.float32)
    own = np.concatenate([band(0.0, 5.0, 1.25), band(5.0, 2.5, 1.0), band(1.25, 1.0, 0.625), eye], 1)
    above = np.concatenate([eye, none, none, none], 1)
    return np.concatenate([own, above], 0)


def back(place, counts, mean, scale, bins, mask, atlas, halos):
    f32, bf16, i32 = jnp.float32, jnp.bfloat16, jnp.int32
    vmem = pl.BlockSpec(memory_space=pltpu.VMEM)
    sds = jax.ShapeDtypeStruct
    weights = jnp.asarray(stencil_weights(), bf16)
    return pl.pallas_call(
        back_kernel,
        out_shape=(sds((PH, PL, ROWS, COLS), bf16), sds((3, PH), f32), sds((1, 16), f32)),
        in_specs=[pl.BlockSpec(memory_space=pltpu.SMEM)] + [vmem] * 13,
        out_specs=(vmem, vmem, vmem),
        scratch_shapes=[
            pltpu.VMEM((PH, PL, 32, COLS + 256), bf16),
            pltpu.VMEM((PL, 32, COLS + 256), i32),
            pltpu.VMEM((3, PH, 8, 128), f32),
            pltpu.VMEM((PL, PH * 32, 128), f32),
            pltpu.VMEM((PL, 32, 128), f32),
            pltpu.VMEM((PL + 1, PH * 32, 128), bf16),
            pltpu.VMEM((PL + 1, PH * 24, 128), bf16),
            pltpu.VMEM((PL, PH * 32, 128), f32),
            pltpu.VMEM((PL, PH * 32, 128), f32),
            pltpu.VMEM((PL, PH * 32, 128), f32),
            pltpu.VMEM((PL + 1, PH * 32, 128), f32),
            pltpu.VMEM((2, PL, PH, ROWS, 128), f32),
        ],
        name="fit_and_label",
    )(place, counts, mean, scale, bins, mask, atlas, *halos, weights)


def per_device(bins, mask, atlas, init_mean, init_scale):
    counts, *halos = front(bins, mask, atlas)
    place = jnp.stack(
        [lax.axis_index("gy"), lax.axis_index("gx"), lax.axis_size("gy"), lax.axis_size("gx")]
    ).astype(jnp.int32)
    prob, params, density = back(
        place, counts.reshape(NB // 128, 128), init_mean[:, None], init_scale[:, None], bins, mask, atlas, halos
    )
    return prob, params, density.reshape(-1)


def solution(mesh):
    in_specs = (P(None, "gy", "gx"), P(None, "gy", "gx"), P(None, None, "gy", "gx"), P(), P())
    out_specs = (P(None, None, "gy", "gx"), P(), P(("gy", "gx")))
    return jax.shard_map(
        per_device, mesh=mesh, in_specs=in_specs, out_specs=out_specs, check_vma=False
    )
```

time: 588 us -> 89.7 us (0.15)
  blocking collectives: 449 us -> 0 us
  Pallas kernels: 0 us -> 84.8 us
  other arithmetic: 61.4 us -> 0.62 us
  starting transfers between devices: 32.3 us -> 0 us
  waiting for transfers between devices: 27.2 us -> 0 us
  matrix products: 6.88 us -> 0 us
    psum x5 -> x0, blocking collectives: 367 us -> none  [per_device(): sums = lax.psum(moments(share, centers, mean, var, weight), ('gy', 'gx'))]
    pallas_call x0 -> x2, Pallas kernels: none -> 84.8 us  [the longest x1 44.7 us: back(): pl.pallas_call(back_kernel, out_shape=(sds((PH, PL, ROWS, COLS), bf16), s...]
    unnamed x1 -> x0, blocking collectives: 81.5 us -> none
    reduce_max x9 -> x0, other arithmetic: 35.5 us -> none  [the longest x3 33.8 us: per_device(): q = jax.nn.softmax(unary + BETA * field, axis=0).astype(jnp.bfloat16)]
    ppermute x12 -> x0, starting transfers between devices: 32.3 us -> none  [the longest x6 22.2 us: extended(): before = lax.ppermute(last, axis, up)]
    ppermute x12 -> x0, waiting for transfers between devices: 27.2 us -> none  [the longest x6 25.3 us: extended(): after = lax.ppermute(initial, axis, down)]
    concatenate x3 -> x0, other arithmetic: 8.65 us -> none  [extended(): x = jnp.concatenate([before, x, after], axis=dim)]
    dot_general x4 -> x0, matrix products: 6.88 us -> none  [count_block(): lax.dot_general(high_hot, low_hot, (((1,), (1,)), ((), ())), preferred_el...]
  transfers between devices with their start and end apart: 12 -> 0, of which waited for: 10 -> 0; matrix products, arithmetic and copies ran while one was open for 0% -> 0% of each run, Pallas kernels for 0% -> 0%
where the time goes in v2:
time: 89.7 us; the launch traced here: 89.5 us
  Pallas kernels  84.8 us (95%)
  local copies, waits for them, and re-layouts  3.43 us (4%)
    pallas_call x1, Pallas kernels, back(): pl.pallas_call(back_kernel, out_shape=(sds((PH, PL, ROWS, COLS), bf16), s...  44.7 us
    pallas_call x1, Pallas kernels, front(): pl.pallas_call(front_kernel, out_shape=(sds((64, 64), f32), sds((2, PH, P...  40.2 us

profile of v2, /device:TPU:1, one launch (start us, length us, event | category | flops | bytes accessed | tf_op | source)
XLA Modules:
  0.0 89.5 jit_solution(3285318486422075702)
XLA Ops:
  0.6 0.6 pad_add_fusion.place_ref
  1.3 0.0 copy-start
  1.3 0.7 copy-done
  1.9 0.0 copy-start.1
  1.9 0.7 copy.9.mean_ref
  2.6 0.0 copy-done.1
  2.6 0.7 copy.10.scale_ref
  3.3 40.2 %histogram_and_halo.1 = (f32[64,64]{1,0:T(8,128)}, bf16[2,8,4,8,1024]{4,3,2,1,0:T(8,128)(2,1)}, bf16[2,8,4,16,128]{4,3,2,1,0:T(8,128)(2,1)}, bf16[4,8,4,8,128]{4...) custom-call(s32[4,16,1024]{2,1,0:T(8,128)} %bins_ref.3, ...), custom_call_target="tpu_custom_call" | custom-call | tf_op jit(solution)/shard_map/histogram_and_halo/pallas_call | solution.py:157
  43.4 1.4 %reshape.12.counts_ref = f32[32,128]{1,0:T(8,128)} reshape(f32[64,64]{1,0:T(8,128)} %get-tuple-element.13) | data formatting | bytes 32768 | tf_op jit(solution)/shard_map/reshape | solution.py:444
  44.9 44.7 %fit_and_label.1 = (bf16[8,4,16,1024]{3,2,1,0:T(8,128)(2,1)}, f32[3,8]{1,0:T(4,128)}, f32[1,16]{1,0:T(1,128)}) custom-call(s32[4]{0:T(128)} %pad_add_fusion.place_ref, f32[32,128]{1,0:T(8,128)} %reshape.12.counts_ref, f32[8,1]{1,0:T(8,128)} %copy.9.mean_ref, f32[8,1]{1,0:T(8,128)} %copy.10.scale_ref, s32[4,16,1024]{2,1,0:T(8,128)} %bins_ref.3, ...), custom_call_target="tpu_custom_call" | custom-call | tf_op jit(solution)/shard_map/fit_and_label/pallas_call | solution.py:415
Async XLA Ops:
  1.3 0.7 copy-start
  1.9 0.7 copy-start.1

commit v3 on v2

--- a/solution.py
+++ b/solution.py
@@ -63,6 +63,23 @@
         high[plane * ROWS : (plane + 1) * ROWS, :] = jnp.where(keep, b // 64, 255).astype(jnp.float32)
         low[plane * ROWS : (plane + 1) * ROWS, :] = (b & 63).astype(jnp.float32)
 
+    levels = lax.broadcasted_iota(jnp.int32, (64, COLS), 0).astype(jnp.float32).astype(jnp.bfloat16)
+    one, zero = jnp.ones((), jnp.bfloat16), jnp.zeros((), jnp.bfloat16)
+    total[...] = jnp.zeros_like(total)
+
+    def count(step, carry):
+        hot = [], []
+        for row in range(8):
+            for digits, out in zip((high, low), hot):
+                wide = jnp.broadcast_to(digits[pl.ds(step * 8 + row, 1), :], (64, COLS))
+                out.append(jnp.where(wide.astype(jnp.bfloat16) == levels, one, zero))
+        total[...] += lax.dot_general(
+            jnp.concatenate(hot[0], axis=1), jnp.concatenate(hot[1], axis=1),
+            (((1,), (1,)), ((), ())), preferred_element_type=jnp.float32,
+        )
+        return carry
+
+    lax.fori_loop(0, PL * ROWS // 16, count, 0)
     pl.semaphore_wait(barrier, len(partners))
 
     bottom, top = pl.ds(ROWS - 8, 8), pl.ds(0, 8)
@@ -91,21 +108,7 @@
     for copy in copies:
         copy.start()
 
-    levels = lax.broadcasted_iota(jnp.int32, (64, COLS), 0).astype(jnp.float32).astype(jnp.bfloat16)
-    one, zero = jnp.ones((), jnp.bfloat16), jnp.zeros((), jnp.bfloat16)
-    total[...] = jnp.zeros_like(total)
-
-    def count(r, carry):
-        h = jnp.broadcast_to(high[pl.ds(r, 1), :], (64, COLS)).astype(jnp.bfloat16)
-        l = jnp.broadcast_to(low[pl.ds(r, 1), :], (64, COLS)).astype(jnp.bfloat16)
-        hot_h = jnp.where(h == levels, one, zero)
-        hot_l = jnp.where(l == levels, one, zero)
-        total[...] += lax.dot_general(
-            hot_h, hot_l, (((1,), (1,)), ((), ())), preferred_element_type=jnp.float32
-        )
-        return carry
-
-    lax.fori_loop(0, PL * ROWS, count, 0)
+    lax.fori_loop(PL * ROWS // 16, PL * ROWS // 8, count, 0)
     mine = total[...]
     half[...] = mine
 
@@ -188,10 +191,12 @@
     )(bins, mask, atlas)
 
 
-def fit(counts_ref, mean, scale):
-    wide = [jnp.broadcast_to(counts_ref[r : r + 1, :], (PH, 128)) for r in range(NB // 128)]
+def fit(table, mean, scale):
+    wide = [jnp.broadcast_to(table[r : r + 1, :], (PH, 128)) for r in range(NB // 128)]
     counts = jnp.concatenate(wide, axis=1)
-    centers = (lax.broadcasted_iota(jnp.int32, (PH, NB), 1).astype(jnp.float32) + 0.5) / NB
+    at = lax.broadcasted_iota(jnp.int32, (PH, NB), 1)
+    bins = 64 * (at // 128) + (at & 63) + NB // 128 * (at & 64)
+    centers = (bins.astype(jnp.float32) + 0.5) / NB
     first_w = counts * centers
     second_w = first_w * centers
     var = scale * scale
@@ -210,26 +215,39 @@
     return mean, var, weight
 
 
-def softmax_into(t, r_mask):
-    top = functools.reduce(jnp.maximum, t)
-    e = [jnp.exp2(v - top) for v in t]
-    inv = jnp.where(r_mask > 0.0, 1.0 / functools.reduce(jnp.add, e), 0.0)
+def total_of(parts, op):
+    while len(parts) > 1:
+        parts = [op(a, b) for a, b in zip(parts[::2], parts[1::2])]
+    return parts[0]
+
+
+def softmax_into(t, mask):
+    e = [jnp.exp2(v) for v in t]
+    inv = mask / total_of(e, jnp.add)
     return [v * inv for v in e]
 
 
 def back_kernel(
-    place_ref, counts_ref, mean_ref, scale_ref, bins_ref, mask_ref, atlas_ref,
+    counts_ref, mean_ref, scale_ref, bins_ref, mask_ref, atlas_ref,
     rows_a, side_a, corner_a, rows_c, side_c, corner_c, w_ref,
     prob_ref, params_ref, density_ref,
-    apad, cpad, coef, uns, msk, held, held24, pa, pb, pd, ps, kept,
+    table, apad, cpad, coef, uns, msk, held, held24, pa, pb, pd, across, kept,
 ):
     f32, bf16 = jnp.float32, jnp.bfloat16
-    gy, gx = place_ref[0], place_ref[1]
-    ny, nx = place_ref[2], place_ref[3]
-
-    row = counts_ref[pl.ds(gy, 1), :] * place_scale(bins_ref)
-    density_ref[...] = pltpu.roll(jnp.broadcast_to(row, (8, 128)), lax.rem(128 - gx * 16, 128), 1)[0:1, 0:16]
-    mean, var, weight = fit(counts_ref, mean_ref[...], scale_ref[...])
+    gy, gx = lax.axis_index("gy"), lax.axis_index("gx")
+    ny, nx = lax.axis_size("gy"), lax.axis_size("gx")
+
+    table[...] = jnp.concatenate([counts_ref[0:32, :], counts_ref[32:64, :]], axis=1)
+    start = 2 * gy + gx // 4
+    row = table[pl.ds(lax.rem(start, 32), 1), :] * place_scale(bins_ref)
+    skip = start // 32 * 64 + lax.rem(gx, 4) * 16
+    density_ref[...] = pltpu.roll(jnp.broadcast_to(row, (8, 128)), lax.rem(128 - skip, 128), 1)[0:1, 0:16]
+    phase = lax.broadcasted_iota(jnp.int32, (PH, 1), 0)
+    mean, scale = jnp.zeros((PH, 1), f32), jnp.zeros((PH, 1), f32)
+    for k in range(PH):
+        mean = jnp.where(phase == k, mean_ref[k], mean)
+        scale = jnp.where(phase == k, scale_ref[k], scale)
+    mean, var, weight = fit(table, mean, scale)
     lane = lax.broadcasted_iota(jnp.int32, (PH, 128), 1)
     diag = lane == lax.broadcasted_iota(jnp.int32, (PH, 128), 0)
     for n, column in enumerate((mean, var, weight)):
@@ -270,9 +288,6 @@
     cpad[:, 24:32, 0:128] = jnp.where(has_down & has_left, corner_c[2], 0)
     cpad[:, 24:32, over] = jnp.where(has_down & has_right, corner_c[3], 0)
 
-    held[PL] = jnp.zeros_like(held[PL])
-    held24[PL] = jnp.zeros_like(held24[PL])
-    ps[0] = jnp.zeros_like(ps[0])
     for ref in (pa, pb, pd):
         for plane in range(PL):
             ref[plane, 0:8] = jnp.zeros((8, 128), f32)
@@ -280,45 +295,53 @@
     beta = BETA / 5.0 * LOG2E
     at = lax.broadcasted_iota(jnp.int32, (8, 128), 1)
 
-    def spread_sums(src, per, lead):
-        def plane_dot(plane, carry):
-            both = jnp.concatenate([src[plane], src[plane + 1]], axis=1)
-            out = jnp.dot(both, w_ref[...], preferred_element_type=f32)
-            span = pl.ds(lead, per)
-            pa[plane, span, :] = out[:, 0:128]
-            pb[plane, span, :] = out[:, 128:256]
-            pd[plane, span, :] = out[:, 256:384]
-            ps[plane + 1, span, :] = out[:, 384:512]
-            return carry
-
-        lax.fori_loop(0, PL, plane_dot, 0)
-
-    def update(plane, start, u_start, m_start, per):
+    def spread_sums(src, per, lead, pair):
+        both = jnp.concatenate([src[2 * pair], src[2 * pair + 1]], axis=1)
+        out = jnp.dot(both, w_ref[...], preferred_element_type=f32)
+        span = pl.ds(lead, per)
+        for i in range(2):
+            for n, ref in enumerate((pa, pb, pd)):
+                m = 3 * i + n
+                ref[2 * pair + i, span, :] = out[:, 128 * m : 128 * m + 128]
+
+    def update(side, plane, start, u_start, m_start, per):
         t = []
         for k in range(PH):
             r = k * per + start
-            total = pa[plane, pl.ds(r, 8), :] + ps[plane, pl.ds(r, 8), :]
+            total = pa[plane, pl.ds(r, 8), :]
+            if plane in (1, 2):
+                total = total + across[side, 2 - plane, pl.ds(r, 8), :]
             total = total + (pb[plane, pl.ds(r - 1, 8), :] + pb[plane, pl.ds(r + 1, 8), :])
             total = total + (pd[plane, pl.ds(r - 2, 8), :] + pd[plane, pl.ds(r + 2, 8), :])
             t.append(uns[plane, pl.ds(k * 32 + u_start, 8), :] + beta * total)
         return softmax_into(t, msk[plane, pl.ds(m_start, 8), :])
 
+    def store(side, ref, plane, row, lead, both):
+        both = both.astype(bf16)
+        ref[plane, pl.ds(row, 16), :] = both
+        if plane in (1, 2):
+            across[side, plane - 1, pl.ds(row + lead, 16), :] = 5.0 * both.astype(f32)
+
     def chunk(c, carry):
         turn = 12 * c + 6
-        from_right = at < 128 - turn - 0
+        from_right = at < 128 - turn
 
         def moved(a, b):
             return pltpu.roll(jnp.where(from_right, b, a), turn, 1)
 
         tile_a = pl.ds(pl.multiple_of(c * 128, 128), 128)
         tile_b = pl.ds(pl.multiple_of((c + 1) * 128, 128), 128)
-
-        def begin(plane, carry):
+        wide_right = jnp.concatenate([from_right, from_right], axis=0)
+
+        def begin(plane):
             for pair in range(2):
                 outs = []
                 rows16 = pl.ds(pair * 16, 16)
-                left = [apad[k, plane, rows16, tile_a].astype(f32) for k in range(PH)]
-                right = [apad[k, plane, rows16, tile_b].astype(f32) for k in range(PH)]
+                prior = []
+                for k in range(PH):
+                    one = apad[k, plane, rows16, tile_a].astype(f32)
+                    two = apad[k, plane, rows16, tile_b].astype(f32)
+                    prior.append(jnp.where(wide_right, two, one))
                 for sub in range(2):
                     g = pair * 16 + sub * 8
                     s8 = slice(sub * 8, sub * 8 + 8)
@@ -329,47 +352,39 @@
                     s = ((cd & (NB - 1)).astype(f32) + 0.5) * (1.0 / NB)
                     t = []
                     for k in range(PH):
-                        prior = moved(left[k][s8], right[k][s8])
                         d = s - coef[0, k]
-                        u = (coef[1, k] - d * d * coef[2, k]) + prior * LOG2E
-                        u = jnp.where(keep, u, 0.0)
-                        uns[plane, pl.ds(k * 32 + g, 8), :] = u
+                        u = (coef[1, k] - d * d * coef[2, k]) + pltpu.roll(prior[k][s8], turn, 1) * LOG2E
                         t.append(u)
+                    top = total_of(t, jnp.maximum)
+                    t = [u - top for u in t]
+                    for k in range(PH):
+                        uns[plane, pl.ds(k * 32 + g, 8), :] = t[k]
                     outs.append(softmax_into(t, m))
                 for k in range(PH):
-                    both = jnp.concatenate([outs[0][k], outs[1][k]], axis=0)
-                    held[plane, pl.ds(k * 32 + pair * 16, 16), :] = both.astype(bf16)
-            return carry
-
-        lax.fori_loop(0, PL, begin, 0)
-
-        def store24(plane, outs):
+                    store(0, held, plane, k * 32 + pair * 16, 0, jnp.concatenate([outs[0][k], outs[1][k]], axis=0))
+
+        def store24(side, plane, outs):
             flat = [outs[i][k] for k in range(PH) for i in range(3)]
             for f in range(0, 3 * PH, 2):
-                both = jnp.concatenate([flat[f], flat[f + 1]], axis=0)
-                held24[plane, pl.ds(f * 8, 16), :] = both.astype(bf16)
-
-        spread_sums(held, 256, 0)
-
-        def second(plane, carry):
-            store24(plane, [update(plane, 4 + 8 * i, 4 + 8 * i, 4 + 8 * i, 32) for i in range(3)])
-            return carry
-
-        lax.fori_loop(0, PL, second, 0)
-        spread_sums(held24, 192, 8)
-
-        def third(plane, carry):
-            store24(plane, [update(plane, 8 + 8 * i, 4 + 8 * i, 4 + 8 * i, 24) for i in range(3)])
-            return carry
-
-        lax.fori_loop(0, PL, third, 0)
-        spread_sums(held24, 192, 8)
+                store(side, held24, plane, f * 8, 8, jnp.concatenate([flat[f], flat[f + 1]], axis=0))
+
+        for plane in range(PL):
+            begin(plane)
+        for pair in range(PL // 2):
+            spread_sums(held, 256, 0, pair)
+        for plane in range(PL):
+            store24(1, plane, [update(0, plane, 4 + 8 * i, 4 + 8 * i, 4 + 8 * i, 32) for i in range(3)])
+        for pair in range(PL // 2):
+            spread_sums(held24, 192, 8, pair)
+        for plane in range(PL):
+            store24(0, plane, [update(1, plane, 8 + 8 * i, 4 + 8 * i, 4 + 8 * i, 24) for i in range(3)])
+        for pair in range(PL // 2):
+            spread_sums(held24, 192, 8, pair)
         slot = lax.rem(c, 2)
         before = at < STEP + 12 - 12 * c
         tile_out = pl.ds(pl.multiple_of(jnp.maximum(c - 1, 0) * 128, 128), 128)
-
-        def last(plane, carry):
-            outs = [update(plane, 8 + 4 + 8 * i, 8 + 8 * i, 8 + 8 * i, 24) for i in range(2)]
+        for plane in range(PL):
+            outs = [update(0, plane, 8 + 4 + 8 * i, 8 + 8 * i, 8 + 8 * i, 24) for i in range(2)]
             for k in range(PH):
                 full = []
                 for i in range(2):
@@ -378,9 +393,6 @@
                     kept[slot, plane, k, pl.ds(8 * i, 8), :] = v
                     full.append(jnp.where(before, old, v))
                 prob_ref[k, plane, :, tile_out] = jnp.concatenate(full, axis=0).astype(bf16)
-            return carry
-
-        lax.fori_loop(0, PL, last, 0)
         return carry
 
     lax.fori_loop(0, CHUNKS, chunk, 0)
@@ -401,48 +413,45 @@
             out[d == n] = v
         return out
 
+    flat, one, two = band(0.0, 5.0, 1.25), band(5.0, 2.5, 1.0), band(1.25, 1.0, 0.625)
     eye, none = band(5.0), np.zeros((128, 128), np.float32)
-    own = np.concatenate([band(0.0, 5.0, 1.25), band(5.0, 2.5, 1.0), band(1.25, 1.0, 0.625), eye], 1)
-    above = np.concatenate([eye, none, none, none], 1)
-    return np.concatenate([own, above], 0)
-
-
-def back(place, counts, mean, scale, bins, mask, atlas, halos):
+    upper = np.concatenate([flat, one, two, eye, none, none], 1)
+    lower = np.concatenate([eye, none, none, flat, one, two], 1)
+    return np.concatenate([upper, lower], 0)
+
+
+def back(counts, mean, scale, bins, mask, atlas, halos):
     f32, bf16, i32 = jnp.float32, jnp.bfloat16, jnp.int32
-    vmem = pl.BlockSpec(memory_space=pltpu.VMEM)
+    vmem, smem = pl.BlockSpec(memory_space=pltpu.VMEM), pl.BlockSpec(memory_space=pltpu.SMEM)
     sds = jax.ShapeDtypeStruct
     weights = jnp.asarray(stencil_weights(), bf16)
     return pl.pallas_call(
         back_kernel,
         out_shape=(sds((PH, PL, ROWS, COLS), bf16), sds((3, PH), f32), sds((1, 16), f32)),
-        in_specs=[pl.BlockSpec(memory_space=pltpu.SMEM)] + [vmem] * 13,
+        in_specs=[vmem, smem, smem] + [vmem] * 10,
         out_specs=(vmem, vmem, vmem),
         scratch_shapes=[
+            pltpu.VMEM((NB // 128, 128), f32),
             pltpu.VMEM((PH, PL, 32, COLS + 256), bf16),
             pltpu.VMEM((PL, 32, COLS + 256), i32),
             pltpu.VMEM((3, PH, 8, 128), f32),
             pltpu.VMEM((PL, PH * 32, 128), f32),
             pltpu.VMEM((PL, 32, 128), f32),
-            pltpu.VMEM((PL + 1, PH * 32, 128), bf16),
-            pltpu.VMEM((PL + 1, PH * 24, 128), bf16),
+            pltpu.VMEM((PL, PH * 32, 128), bf16),
+            pltpu.VMEM((PL, PH * 24, 128), bf16),
             pltpu.VMEM((PL, PH * 32, 128), f32),
             pltpu.VMEM((PL, PH * 32, 128), f32),
             pltpu.VMEM((PL, PH * 32, 128), f32),
-            pltpu.VMEM((PL + 1, PH * 32, 128), f32),
+            pltpu.VMEM((2, 2, PH * 32, 128), f32),
             pltpu.VMEM((2, PL, PH, ROWS, 128), f32),
         ],
         name="fit_and_label",
-    )(place, counts, mean, scale, bins, mask, atlas, *halos, weights)
+    )(counts, mean, scale, bins, mask, atlas, *halos, weights)
 
 
 def per_device(bins, mask, atlas, init_mean, init_scale):
     counts, *halos = front(bins, mask, atlas)
-    place = jnp.stack(
-        [lax.axis_index("gy"), lax.axis_index("gx"), lax.axis_size("gy"), lax.axis_size("gx")]
-    ).astype(jnp.int32)
-    prob, params, density = back(
-        place, counts.reshape(NB // 128, 128), init_mean[:, None], init_scale[:, None], bins, mask, atlas, halos
-    )
+    prob, params, density = back(counts, init_mean, init_scale, bins, mask, atlas, halos)
     return prob, params, density.reshape(-1)
 
 

time: 89.7 us -> 58.7 us (0.65)
  Pallas kernels: 84.8 us -> 57.9 us
  local copies, waits for them, and re-layouts: 3.43 us -> 0 us
    pallas_call x1, Pallas kernels: 44.7 us -> 18.2 us  [back(): pl.pallas_call(back_kernel, out_shape=(sds((PH, PL, ROWS, COLS), bf16), s...]
    reshape x1 -> x0, local copies, waits for them, and re-layouts: 1.43 us -> none  [per_device(): counts.reshape(NB // 128, 128)]
    broadcast_in_dim x2 -> x0, local copies, waits for them, and re-layouts: 1.34 us -> none  [the longest x1 0.67 us: per_device(): init_scale[:, None]]
where the time goes in v3:
time: 58.7 us; the launch traced here: 58.6 us
  Pallas kernels  57.9 us (99%)
  between operations  0.64 us (1%)
    pallas_call x1, Pallas kernels, front(): pl.pallas_call(front_kernel, out_shape=(sds((64, 64), f32), sds((2, PH, P...  39.8 us
    pallas_call x1, Pallas kernels, back(): pl.pallas_call(back_kernel, out_shape=(sds((PH, PL, ROWS, COLS), bf16), s...  18.2 us

profile of v3, /device:TPU:1, one launch (start us, length us, event | category | flops | bytes accessed | tf_op | source)
XLA Modules:
  0.0 58.6 jit_solution(14884279798919104810)
XLA Ops:
  0.6 39.8 %histogram_and_halo.1 = (f32[64,64]{1,0:T(8,128)}, bf16[2,8,4,8,1024]{4,3,2,1,0:T(8,128)(2,1)}, bf16[2,8,4,16,128]{4,3,2,1,0:T(8,128)(2,1)}, bf16[4,8,4,8,128]{4...) custom-call(s32[4,16,1024]{2,1,0:T(8,128)} %bins_ref.3, ...), custom_call_target="tpu_custom_call" | custom-call | tf_op jit(solution)/shard_map/histogram_and_halo/pallas_call | solution.py:160
  40.4 18.2 %fit_and_label.1 = (bf16[8,4,16,1024]{3,2,1,0:T(8,128)(2,1)}, f32[3,8]{1,0:T(4,128)}, f32[1,16]{1,0:T(1,128)}) custom-call(f32[64,64]{1,0:T(8,128)} %get-tuple-element.13.counts_ref, f32[8]{0:T(128)} %mean_ref.1, f32[8]{0:T(128)} %scale_ref.1, s32[4,16,1024]{2,1,0:T(8,128)} %bins_ref.3, s32[4,16,1024]{2,1,0:T(8,128)} %mask_ref.3, ...), custom_call_target="tpu_custom_call" | custom-call | tf_op jit(solution)/shard_map/fit_and_label/pallas_call | solution.py:428

commit v4 on v3

--- a/solution.py
+++ b/solution.py
@@ -21,6 +21,8 @@
 ROWS = 16
 COLS = 1024
 STEP = 116
+HALO = 6
+SHARE = 3, 1, 2, 4, 0
 CHUNKS = 9
 NX, NY, NZ = 4, 4, 8
 
@@ -34,8 +36,8 @@
 def front_kernel(
     bins_ref, mask_ref, atlas_ref,
     counts_ref, rows_a, side_a, corner_a, rows_c, side_c, corner_c,
-    code, high, low, half, core_in, x_in, y_in, z_in, stage, total,
-    halo_send, halo_recv, sum_send, sum_recv,
+    code, high, low, edges, strips_a, strips_c, half, core_in, x_in, y_in, z_in, stage, total,
+    edge_sem, halo_send, halo_recv, sum_send, sum_recv,
 ):
     ny, nx = lax.axis_size("gy"), lax.axis_size("gx")
     gy, gx = lax.axis_index("gy"), lax.axis_index("gx")
@@ -56,6 +58,12 @@
     for device in partners:
         pl.semaphore_signal(barrier, inc=1, device_id=device, device_id_type=MESH)
 
+    edge_copies = [
+        pltpu.make_async_copy(atlas_ref.at[:, :, :, pl.ds(lane, 128)], edges.at[n], edge_sem.at[n])
+        for n, lane in enumerate((0, COLS - 128))
+    ]
+    for copy in edge_copies:
+        copy.start()
     code[...] = bins_ref[...] + NB * mask_ref[...]
     for plane in range(PL):
         b = bins_ref[plane]
@@ -80,32 +88,70 @@
         return carry
 
     lax.fori_loop(0, PL * ROWS // 16, count, 0)
+
+    for copy in edge_copies:
+        copy.wait()
+    place = lax.broadcasted_iota(jnp.int32, (8, 128), 1) // 8
+    for n in range(4):
+        row, side = 8 * (n // 2), n % 2
+        tiles = []
+        for tile in range(2):
+            acc = jnp.zeros((8, 128), jnp.float32)
+            for i in range(16):
+                k, plane = divmod(16 * tile + i, PL)
+                v = edges[side, k, plane].astype(jnp.float32)[row : row + 8]
+                acc = jnp.where(place == i, pltpu.roll(v, (8 * i + 8 * side) % 128, 1), acc)
+            tiles.append(acc)
+        strips_a[n] = jnp.concatenate(tiles, axis=0).astype(jnp.bfloat16)
+        acc = jnp.zeros((8, 128), jnp.int32)
+        for plane in range(PL):
+            v = code[plane, row : row + 8, (COLS - 128) * side : (COLS - 128) * side + 128]
+            acc = jnp.where(place == plane, pltpu.roll(v, 8 * plane + 8 * side, 1), acc)
+        strips_c[n] = acc
     pl.semaphore_wait(barrier, len(partners))
 
-    bottom, top = pl.ds(ROWS - 8, 8), pl.ds(0, 8)
+    bottom, top = pl.ds(ROWS - HALO, HALO), pl.ds(0, HALO)
     last, first = pl.ds(COLS - 128, 128), pl.ds(0, 128)
+
+    def block(r, c):
+        return atlas_ref.at[:, :, r, c], code.at[:, r, c]
+
     every, wide = pl.ds(0, ROWS), pl.ds(0, COLS)
-    plan = [
-        ((up, gx), top, wide, rows_a.at[1], rows_c.at[1]),
-        ((down, gx), bottom, wide, rows_a.at[0], rows_c.at[0]),
-        ((gy, left), every, first, side_a.at[1], side_c.at[1]),
-        ((gy, right), every, last, side_a.at[0], side_c.at[0]),
-        ((up, left), top, first, corner_a.at[3], corner_c.at[3]),
-        ((up, right), top, last, corner_a.at[2], corner_c.at[2]),
-        ((down, left), bottom, first, corner_a.at[1], corner_c.at[1]),
-        ((down, right), bottom, last, corner_a.at[0], corner_c.at[0]),
+    plan = []
+    for k in range(PH):
+        for n, device, r in ((1, (up, gx), top), (0, (down, gx), bottom)):
+            plan.append((device, (atlas_ref.at[k, :, r, wide],), (rows_a.at[n, k],)))
+    for ps in (pl.ds(0, PL // 2), pl.ds(PL // 2, PL // 2)):
+        for n, device, r in ((1, (up, gx), top), (0, (down, gx), bottom)):
+            plan.append((device, (code.at[ps, r, wide],), (rows_c.at[n, ps],)))
+    pieces = len(plan)
+    plan += [
+        ((gy, left), block(every, first), (side_a.at[1], side_c.at[1])),
+        ((gy, right), block(every, last), (side_a.at[0], side_c.at[0])),
     ]
+    diagonal = (up, left), (up, right), (down, left), (down, right)
+    for n, device in enumerate(diagonal):
+        to = corner_a.at[3 - n], corner_c.at[3 - n]
+        plan.append((device, (strips_a.at[n], strips_c.at[n]), to))
     copies = []
-    for n, (device, r, c, to_a, to_c) in enumerate(plan):
-        for m, (src, dst) in enumerate(((atlas_ref.at[:, :, r, c], to_a), (code.at[:, r, c], to_c))):
+    for device, give, take in plan:
+        for src, dst in zip(give, take):
             copies.append(
                 pltpu.make_async_remote_copy(
                     src_ref=src, dst_ref=dst,
-                    send_sem=halo_send.at[2 * n + m], recv_sem=halo_recv.at[2 * n + m],
+                    send_sem=halo_send.at[len(copies)], recv_sem=halo_recv.at[len(copies)],
                     device_id=device, device_id_type=MESH,
                 )
             )
-    for copy in copies:
+    queue = list(copies[:pieces])
+
+    def send(count):
+        for copy in queue[: 2 * count]:
+            copy.start()
+        del queue[: 2 * count]
+
+    send(SHARE[0])
+    for copy in copies[pieces:]:
         copy.start()
 
     lax.fori_loop(PL * ROWS // 16, PL * ROWS // 8, count, 0)
@@ -123,17 +169,19 @@
     done = []
     copy = exchange(half.at[give_rows], core_in, (gy, other), 0)
     copy.start()
+    send(SHARE[1])
     copy.wait_recv()
     done.append(copy)
     stage[0] = half[keep_rows, :] + core_in[...]
     n = 1
-    for level, (group, landing) in enumerate(((along_x, x_in), (along_y, y_in), (along_z, z_in))):
+    for level, (group, landing) in enumerate(((along_x, x_in), (along_z, z_in), (along_y, y_in))):
         now = []
         for i, device in enumerate(group):
             now.append(exchange(stage.at[level], landing.at[i], device, n))
             n += 1
         for copy in now:
             copy.start()
+        send(SHARE[2 + level])
         acc = stage[level]
         for i, copy in enumerate(now):
             copy.wait_recv()
@@ -161,12 +209,12 @@
         front_kernel,
         out_shape=(
             sds((64, 64), f32),
-            sds((2, PH, PL, 8, COLS), bf16),
+            sds((2, PH, PL, HALO, COLS), bf16),
             sds((2, PH, PL, ROWS, 128), bf16),
-            sds((4, PH, PL, 8, 128), bf16),
-            sds((2, PL, 8, COLS), i32),
+            sds((4, 16, 128), bf16),
+            sds((2, PL, HALO, COLS), i32),
             sds((2, PL, ROWS, 128), i32),
-            sds((4, PL, 8, 128), i32),
+            sds((4, 8, 128), i32),
         ),
         in_specs=[vmem, vmem, anywhere],
         out_specs=(vmem,) + (anywhere,) * 6,
@@ -174,6 +222,9 @@
             pltpu.VMEM((PL, ROWS, COLS), i32),
             pltpu.VMEM((PL * ROWS, COLS), f32),
             pltpu.VMEM((PL * ROWS, COLS), f32),
+            pltpu.VMEM((2, PH, PL, ROWS, 128), bf16),
+            pltpu.VMEM((4, 16, 128), bf16),
+            pltpu.VMEM((4, 8, 128), i32),
             pltpu.VMEM((64, 64), f32),
             pltpu.VMEM((32, 64), f32),
             pltpu.VMEM((NX - 1, 32, 64), f32),
@@ -181,8 +232,9 @@
             pltpu.VMEM((NZ - 1, 32, 64), f32),
             pltpu.VMEM((4, 32, 64), f32),
             pltpu.VMEM((64, 64), f32),
-            pltpu.SemaphoreType.DMA((16,)),
-            pltpu.SemaphoreType.DMA((16,)),
+            pltpu.SemaphoreType.DMA((2,)),
+            pltpu.SemaphoreType.DMA((2 * sum(SHARE) + 12,)),
+            pltpu.SemaphoreType.DMA((2 * sum(SHARE) + 12,)),
             pltpu.SemaphoreType.DMA((sums,)),
             pltpu.SemaphoreType.DMA((sums,)),
         ],
@@ -267,27 +319,33 @@
             apad[k, plane, 8:24, own] = atlas_ref[k, plane]
             apad[k, plane, 8:24, 0:128] = side_a[0, k, plane]
             apad[k, plane, 8:24, over] = side_a[1, k, plane]
-            apad[k, plane, 0:8, own] = rows_a[0, k, plane]
-            apad[k, plane, 24:32, own] = rows_a[1, k, plane]
-            apad[k, plane, 0:8, 0:128] = corner_a[0, k, plane]
-            apad[k, plane, 0:8, over] = corner_a[1, k, plane]
-            apad[k, plane, 24:32, 0:128] = corner_a[2, k, plane]
-            apad[k, plane, 24:32, over] = corner_a[3, k, plane]
+            apad[k, plane, 8 - HALO : 8, own] = rows_a[0, k, plane]
+            apad[k, plane, 24 : 24 + HALO, own] = rows_a[1, k, plane]
         return carry
 
     lax.fori_loop(0, PH, fill, 0)
+    corners = [corner_a[n].astype(f32) for n in range(4)]
+    for n in range(4):
+        rows, lanes = pl.ds(24 * (n // 2), 8), (pl.ds(0, 128), over)[n % 2]
+        for k in range(PH):
+            for plane in range(PL):
+                tile, i = divmod(k * PL + plane, 16)
+                v = corners[n][8 * tile : 8 * tile + 8]
+                v = pltpu.roll(v, (120 * (1 - n % 2) + 128 - 8 * i) % 128, 1)
+                apad[k, plane, rows, lanes] = v.astype(bf16)
     has_up, has_down = gy > 0, gy < ny - 1
     has_left, has_right = gx > 0, gx < nx - 1
     cpad[:, 8:24, own] = bins_ref[...] + NB * mask_ref[...]
     cpad[:, 8:24, 0:128] = jnp.where(has_left, side_c[0], 0)
     cpad[:, 8:24, over] = jnp.where(has_right, side_c[1], 0)
-    cpad[:, 0:8, own] = jnp.where(has_up, rows_c[0], 0)
-    cpad[:, 24:32, own] = jnp.where(has_down, rows_c[1], 0)
-    cpad[:, 0:8, 0:128] = jnp.where(has_up & has_left, corner_c[0], 0)
-    cpad[:, 0:8, over] = jnp.where(has_up & has_right, corner_c[1], 0)
-    cpad[:, 24:32, 0:128] = jnp.where(has_down & has_left, corner_c[2], 0)
-    cpad[:, 24:32, over] = jnp.where(has_down & has_right, corner_c[3], 0)
-
+    cpad[:, 8 - HALO : 8, own] = jnp.where(has_up, rows_c[0], 0)
+    cpad[:, 24 : 24 + HALO, own] = jnp.where(has_down, rows_c[1], 0)
+    for n in range(4):
+        valid = (has_up, has_down)[n // 2] & (has_left, has_right)[n % 2]
+        rows, lanes = pl.ds(24 * (n // 2), 8), (pl.ds(0, 128), over)[n % 2]
+        for plane in range(PL):
+            v = pltpu.roll(corner_c[n], (120 * (1 - n % 2) + 128 - 8 * plane) % 128, 1)
+            cpad[plane, rows, lanes] = jnp.where(valid, v, 0)
     for ref in (pa, pb, pd):
         for plane in range(PL):
             ref[plane, 0:8] = jnp.zeros((8, 128), f32)

time: 58.7 us -> 50.7 us (0.86)
  Pallas kernels: 57.9 us -> 49.9 us
    pallas_call x1, Pallas kernels: 39.8 us -> 31.7 us  [front(): pl.pallas_call(front_kernel, out_shape=(sds((64, 64), f32), sds((2, PH, P...]
where the time goes in v4:
time: 50.7 us; the launch traced here: 50.5 us
  Pallas kernels  49.9 us (98%)
  between operations  0.64 us (1%)
    pallas_call x1, Pallas kernels, front(): pl.pallas_call(front_kernel, out_shape=(sds((64, 64), f32), sds((2, PH, P...  31.7 us
    pallas_call x1, Pallas kernels, back(): pl.pallas_call(back_kernel, out_shape=(sds((PH, PL, ROWS, COLS), bf16), s...  18.2 us

profile of v4, /device:TPU:1, one launch (start us, length us, event | category | flops | bytes accessed | tf_op | source)
XLA Modules:
  0.0 50.5 jit_solution(12385071468096282271)
XLA Ops:
  0.6 31.7 %histogram_and_halo.1 = (f32[64,64]{1,0:T(8,128)}, bf16[2,8,4,6,1024]{4,3,2,1,0:T(8,128)(2,1)}, bf16[2,8,4,16,128]{4,3,2,1,0:T(8,128)(2,1)}, bf16[4,16,128]{2,1,...) custom-call(s32[4,16,1024]{2,1,0:T(8,128)} %bins_ref.3, ...), custom_call_target="tpu_custom_call" | custom-call | tf_op jit(solution)/shard_map/histogram_and_halo/pallas_call | solution.py:208
  32.3 18.2 %fit_and_label.1 = (bf16[8,4,16,1024]{3,2,1,0:T(8,128)(2,1)}, f32[3,8]{1,0:T(4,128)}, f32[1,16]{1,0:T(1,128)}) custom-call(f32[64,64]{1,0:T(8,128)} %get-tuple-element.13.counts_ref, f32[8]{0:T(128)} %mean_ref.1, f32[8]{0:T(128)} %scale_ref.1, s32[4,16,1024]{2,1,0:T(8,128)} %bins_ref.3, s32[4,16,1024]{2,1,0:T(8,128)} %mask_ref.3, ...), custom_call_target="tpu_custom_call" | custom-call | tf_op jit(solution)/shard_map/fit_and_label/pallas_call | solution.py:486
